TPU v7x, 128 devices: a whole 4x4x4 slice. The times are simulated.
128 devices in a mesh: band: 4 (over y), sector: 32 (over x, z, core).
Axes of the slice: x: 4, y: 4, z: 4, core: 2. Of those that a mesh axis runs over, the one named last changes fastest.
Arguments:
- grid_cells: bfloat16 [8192, 128, 128], P(('band', 'sector')), may hold values from -6 to 6
- remap_weight: bfloat16 [8192, 2, 128, 128], P(('band', 'sector')), may hold values from -0.15625 to 0.15625
- remap_dest: int32 [8192, 2], P(('band', 'sector')), may hold values from 0 to 127, all different within a row; in each aligned block of 64 rows (0 to 63, 64 to 127, ...) at most 2 rows name the same one
- remap_tile: int32 [8192, 2], P(('band', 'sector')), may hold values from 0 to 11
- w_embed: bfloat16 [128, 1024], replicated, may hold values from -0.5 to 0.5
- norm_gain: float32 [1024], replicated, may hold values from 0.25 to 1.75
- w_query: bfloat16 [1024, 1024], replicated
- w_key: bfloat16 [1024, 1024], replicated
- w_value: bfloat16 [1024, 1024], replicated, may hold values from -0.1875 to 0.1875
- w_out: bfloat16 [1024, 1024], replicated, may hold values from -0.1875 to 0.1875
- neighbours: int32 [8, 192, 9], P('band', 'sector'), may hold values from 0 to 1535, as said below
Outputs:
- layer_out: bfloat16 [8, 192, 128, 1024], P('band', 'sector')
Inputs may be any that keep to these rules, and one draw needn't show every extreme that they name: `remap_dest`: within the row-blocks of one device, no device number is named more than 2 times; some number is named exactly 2 times. `neighbours`: entry 0 of a tile is the tile itself; every entry lies at most one tile row and one tile column away, columns counted around the sphere, rows never past the first or last; entries may repeat.
All inputs are finite; a program needn't handle non-finite values.
Results may differ from a plain program's by a relative error of at most 0.0064.
Values may be sent and summed in bfloat16 or wider, within the bound.
A program may use at most 256 MiB of HBM per device.

v0:
```python
import math

import jax
import jax.numpy as jnp
from jax import lax
from jax.sharding import PartitionSpec as P

HEADS = 16
HD = 64


def padded(block, sides, width, periodic):
    for axis, dim in sides:
        count = lax.axis_size(axis)
        forward = [(i, i + 1) for i in range(count - 1)]
        if periodic:
            forward.append((count - 1, 0))
        backward = [(target, source) for source, target in forward]
        low = lax.ppermute(
            lax.slice_in_dim(block, block.shape[dim] - width, None, axis=dim), axis, forward
        )
        high = lax.ppermute(lax.slice_in_dim(block, 0, width, axis=dim), axis, backward)
        block = jnp.concatenate([low, block, high], axis=dim)
    return block


def tile_angles(rows, cols, nrows, ncols, tile):
    place = jnp.arange(tile)
    across = (place // 16).astype(jnp.float32)
    along = (place % 16).astype(jnp.float32)
    theta = math.pi * (rows[..., None].astype(jnp.float32) + (across + 0.5) * 16.0 / tile) / nrows
    phi = 2.0 * math.pi * (cols[..., None].astype(jnp.float32) + (along + 0.5) / 16.0) / ncols
    return (theta, phi)


def project_heads(weight, tiles):
    full = jnp.einsum("wf,rctw->frct", weight, tiles, preferred_element_type=jnp.float32)
    return full.reshape((HEADS, HD) + full.shape[1:])


def rotate_heads(values, theta, phi):
    quarter = values.shape[1] // 4
    freq = jnp.arange(1, quarter + 1).astype(jnp.float32).reshape((quarter, 1, 1, 1))
    lat_angle = theta[None] * freq
    lon_angle = phi[None] * freq

    def turn(lower, upper, angle):
        cosine = jnp.cos(angle)
        sine = jnp.sin(angle)
        return [lower * cosine - upper * sine, lower * sine + upper * cosine]

    pieces = turn(values[:, :quarter], values[:, quarter : 2 * quarter], lat_angle)
    pieces = pieces + turn(
        values[:, 2 * quarter : 3 * quarter], values[:, 3 * quarter :], lon_angle
    )
    return jnp.concatenate(pieces, axis=1)


def keys_and_values(tiles, theta, phi, w_key, w_value):
    keys = rotate_heads(project_heads(w_key, tiles), theta, phi).astype(jnp.bfloat16)
    values = project_heads(w_value, tiles).astype(jnp.bfloat16)
    return jnp.stack([keys, values], axis=0)


def body(
    grid_cells,
    remap_weight,
    remap_dest,
    remap_tile,
    w_embed,
    norm_gain,
    w_query,
    w_key,
    w_value,
    w_out,
    neighbours,
):
    nband = lax.axis_size("band")
    nsect = lax.axis_size("sector")
    ndev = nband * nsect
    blocks, top, rowcells, tile = remap_weight.shape
    chan = grid_cells.shape[2]
    width = w_embed.shape[1]
    trows, tcols = (neighbours.shape[0], neighbours.shape[1])
    cap = max(2, 2 * blocks * top // ndev)
    items = blocks * top
    parts = jnp.einsum(
        "rkct,rcf->rktf", remap_weight, grid_cells, preferred_element_type=jnp.float32
    )
    parts = parts.astype(jnp.bfloat16).reshape(items, tile, chan)
    dest = remap_dest.reshape(-1)
    local = remap_tile.reshape(-1)
    order = jnp.arange(items)
    earlier = (dest[:, None] == dest[None, :]) & (order[None, :] < order[:, None])
    rank = jnp.sum(earlier.astype(jnp.int32), axis=1)
    slot = dest * cap + rank
    send_parts = jnp.zeros((ndev * cap, tile, chan), jnp.bfloat16).at[slot].set(parts)
    send_ids = jnp.full((ndev * cap,), -1, jnp.int32).at[slot].set(local)
    got_parts, got_ids = (
        lax.all_to_all(send_parts, ("band", "sector"), split_axis=0, concat_axis=0, tiled=True),
        lax.all_to_all(send_ids, ("band", "sector"), split_axis=0, concat_axis=0, tiled=True),
    )
    owned = trows * tcols
    select = (got_ids[None, :] == jnp.arange(owned)[:, None]).astype(jnp.bfloat16)
    remapped = jnp.einsum(
        "ls,stc->ltc", select, got_parts, preferred_element_type=jnp.float32
    ).astype(jnp.bfloat16)
    embedded = jnp.dot(remapped.reshape(-1, chan), w_embed, preferred_element_type=jnp.float32)
    meansq = jnp.mean(embedded * embedded, axis=-1, keepdims=True)
    normed = (embedded * lax.rsqrt(meansq + 1e-05) * norm_gain).astype(jnp.bfloat16)
    band_at = lax.axis_index("band")
    sect_at = lax.axis_index("sector")
    nrows = trows * nband
    ncols = tcols * nsect
    own_rows = band_at * trows + jnp.arange(trows)
    own_cols = sect_at * tcols + jnp.arange(tcols)
    own_theta, own_phi = tile_angles(
        own_rows[:, None] + 0 * own_cols[None, :],
        0 * own_rows[:, None] + own_cols[None, :],
        nrows,
        ncols,
        tile,
    )
    normed_tiles = normed.reshape(trows, tcols, tile, width)
    queries = rotate_heads(project_heads(w_query, normed_tiles), own_theta, own_phi).astype(
        jnp.bfloat16
    )
    queries = queries.reshape(HEADS, HD, owned, tile)
    own_kv = keys_and_values(normed_tiles, own_theta, own_phi, w_key, w_value)
    gathered = padded(own_kv, (("band", 3),), 1, False)
    gathered = padded(gathered, (("sector", 4),), 1, True)
    ext_flat = gathered.reshape(2, HEADS, HD, (trows + 2) * (tcols + 2), tile)
    grow = neighbours // ncols
    gcol = neighbours % ncols
    local_row = grow - band_at * trows + 1
    local_col = jnp.mod(gcol - sect_at * tcols + 1, ncols)
    index = (local_row * (tcols + 2) + local_col).reshape(owned, 9)
    group = 4
    ngroups = owned // group
    index_groups = index.reshape(ngroups, group * 9)

    def attend(inputs):
        which, listed = inputs
        query_heads = lax.dynamic_slice_in_dim(queries, which * group, group, 2)
        chosen = jnp.take(ext_flat, listed, axis=3).reshape(2, HEADS, HD, group, 9, tile)
        scores = jnp.einsum(
            "hdbq,hdbjk->hbqjk", query_heads, chosen[0], preferred_element_type=jnp.float32
        ) / math.sqrt(HD)
        probs = jax.nn.softmax(scores, axis=(-2, -1)).astype(jnp.bfloat16)
        mixed = jnp.einsum(
            "hbqjk,hdbjk->hdbq", probs, chosen[1], preferred_element_type=jnp.float32
        )
        return mixed.astype(jnp.bfloat16)

    attended = lax.map(attend, (jnp.arange(ngroups), index_groups))
    result = jnp.einsum(
        "nhdgq,hde->ngqe",
        attended,
        w_out.reshape(HEADS, HD, width),
        preferred_element_type=jnp.float32,
    )
    result = result.reshape(-1, width) + embedded
    return result.astype(jnp.bfloat16).reshape(trows, tcols, tile, width)


def solution(mesh):
    return jax.shard_map(
        body,
        mesh=mesh,
        in_specs=(
            P(("band", "sector"), None, None),
            P(("band", "sector"), None, None, None),
            P(("band", "sector"), None),
            P(("band", "sector"), None),
            P(),
            P(),
            P(),
            P(),
            P(),
            P(),
            P("band", "sector", None),
        ),
        out_specs=P("band", "sector", None, None),
        check_vma=False,
    )
```

profile of v0, /device:TPU:3, one launch (start us, length us, event | category | flops | bytes accessed | tf_op | source)
XLA Modules:
  0.0 666.8 jit_solution(16584962582459283234)
XLA Ops:
  4.8 10.8 %all-to-all-start = ((s32[128,2,1]{1,2,0:T(1,128)}), s32[128,2,1]{1,2,0:T(1,128)S(1)}, u32[]{:S(2)}, u32[]{:S(2)}) async-start(s32[128,2,1]{1,2,0:T(1,128)} %bitcast.16), calls=%async_computation | async-start | bytes 131072 | tf_op jit(solution)/shard_map/all_to_all | solution.py:101
  15.7 6.1 convolution_convert_fusion
  21.8 5.4 broadcast_in_dim.18
  27.1 19.6 %scatter_fusion = bf16[256,128,128]{2,1,0:T(8,128)(2,1)} fusion(bf16[256,128,128]{2,1,0:T(8,128)(2,1)} %broadcast_in_dim.18, s32[128]{0:T(128)S(1)} %fusion.34, bf16[128,128,128]{2,1,0:T(8,128)(2,1)} %bitcast.141), kind=kCustom, calls=%fused_computation.2 | custom fusion | bytes 12583424 | tf_op jit(solution)/shard_map/scatter | solution.py:97
  46.8 10.5 %all-to-all-start.1 = ((bf16[256,128,128]{2,1,0:T(8,128)(2,1)}), bf16[256,128,128]{2,1,0:T(8,128)(2,1)}, u32[]{:S(2)}, u32[]{:S(2)}) async-start(bf16[256,128,128]{2,1,0:T(8,128)(2,1)} %scatter_fusion), calls=%async_computation.1 | async-start | bytes 16777216 | tf_op jit(solution)/shard_map/all_to_all | solution.py:100
  59.7 97.6 %all-to-all-done.1 = bf16[256,128,128]{2,1,0:T(8,128)(2,1)} async-done(((bf16[256,128,128]{2,1,0:T(8,128)(2,1)}), bf16[256,128,128]{2,1,0:T(8,128)(2,1)}, u32[]{:S(2)}, u32[]{:S(2)}) %all-to-all-start.1) | async-done | bytes 8388640 | tf_op jit(solution)/shard_map/all_to_all | solution.py:100
  157.3 7.9 %fusion.15 = bf16[12,128,128]{2,0,1:T(8,128)(2,1)S(1)} fusion(bf16[256,128,128]{2,1,0:T(8,128)(2,1)} %all-to-all-done.1, s32[256]{0:T(256)S(1)} %eq.39), kind=kOutput, calls=%fused_computation.55 | convolution fusion | flops 100862976 | bytes 8782848 | tf_op jit(solution)/shard_map/ls,stc->ltc/dot_general | solution.py:105
  171.0 4.8 convert_bitcast_fusion
  175.7 4.7 copy.79
  180.5 8.6 %convolution_bitcast_fusion.1 = f32[1024,2,6,128]{0,3,2,1:T(8,128)} fusion(bf16[2,6,128,1024]{3,2,1,0:T(8,128)(2,1)} %bitcast.143, bf16[1024,1024]{1,0:T(8,128)(2,1)} %param.20), kind=kOutput, calls=%fused_computation.34 | convolution fusion | flops 3221225472 | bytes 11534336 | tf_op jit(solution)/shard_map/wf,rctw->frct/dot_general | solution.py:37
  189.1 6.9 %copy.78 = f32[1024,2,6,128]{3,0,2,1:T(8,128)} copy(f32[1024,2,6,128]{0,3,2,1:T(8,128)} %convolution_bitcast_fusion.1) | data formatting | bytes 12582912 | tf_op jit(solution)/shard_map/wf,rctw->frct/dot_general | solution.py:37
  196.0 4.1 fusion.18
  206.1 63.9 %collective-permute-done = bf16[2,16,64,1,6,128]{5,2,1,4,3,0:T(8,128)(2,1)S(1)} collective-permute-done((bf16[2,16,64,1,6,128]{5,2,1,4,3,0:T(8,128)(2,1)S(1)}, bf16[2,16,64,1,6,128]{5,2,1,4,3,0:T(8,128)(2,1)S(1)}, u32[]{:S(2)}, u32[]{:S(2)}) %collective-permute-start) | collective-permute-done | bytes 3145760 | tf_op jit(solution)/shard_map/ppermute | solution.py:19
  270.0 4.0 collective-permute-done.1
  277.0 7.6 %collective-permute-start.2 = (bf16[2,16,64,4,1,128]{5,2,1,4,3,0:T(8,128)(2,1)}, bf16[2,16,64,4,1,128]{5,2,1,4,3,0:T(8,128)(2,1)}, u32[]{:S(2)}, u32[]{:S(2)}) collective-permute-start(bf16[2,16,64,4,1,128]{5,2,1,4,3,0:T(8,128)(2,1)} %get-tuple-element.72), channel_id=1, source_target_pairs={{0,1},{1,2},{2,3},{3,4},{4,5},{5,6},{6,7},{7,8},{8,9},{9,10},{10,1... | collective-permute-start | bytes 6291464 | tf_op jit(solution)/shard_map/ppermute | solution.py:19
  284.7 8.6 %convolution_bitcast_fusion = f32[1024,2,6,128]{0,3,2,1:T(8,128)} fusion(bf16[2,6,128,1024]{3,2,1,0:T(8,128)(2,1)} %bitcast.144, bf16[1024,1024]{1,0:T(8,128)(2,1)} %param.19), kind=kOutput, calls=%fused_computation.33 | convolution fusion | flops 3221225472 | bytes 11534336 | tf_op jit(solution)/shard_map/wf,rctw->frct/dot_general | solution.py:37
  293.4 6.5 copy.80
  299.9 4.1 subtract_convert_fusion.1
  310.4 4.6 pad_maximum_fusion
  315.1 7.0 %copy.85 = bf16[2,16,64,32,128]{4,2,3,1,0:T(8,128)(2,1)} copy(bf16[2,16,64,32,128]{4,2,1,3,0:T(8,128)(2,1)S(1)} %bitcast.135) | data formatting | bytes 33554432 | tf_op jit(solution)/shard_map/while | solution.py:155
  322.1 324.5 %while.10 = (s32[]{:T(128)}, bf16[3,16,64,4,128]{4,2,3,1,0:T(8,128)(2,1)}, s32[3,36]{1,0:T(4,128)S(1)}, bf16[2,16,64,32,128]{4,2,3,1,0:T(8,128)(2,1)}, s32[3]{0:...) while((s32[]{:T(128)}, ...), condition=%wide.region_7.8_spmd, body=%wide.region_4.7_spmd.sunk | while | flops 2510800384 | bytes 285381568 | solution.py:155
  323.4 13.7 %gather_fusion = bf16[36,2,16,64,128]{4,3,2,1,0:T(8,128)(2,1)} fusion(bf16[2,16,64,32,128]{4,2,3,1,0:T(8,128)(2,1)} %get-tuple-element.166, s32[1024]{0:T(1024)S(1)} %pad_clamp_fusion.2), kind=kCustom, calls=%fused_computation.clone.1 | custom fusion | bytes 37748880 | tf_op jit(solution)/shard_map/while/body/eval_jaxpr/jit(_take)/gather | solution.py:145
  337.1 9.7 %select_bitcast_fusion.2 = bf16[2,16,64,36,128]{4,2,1,0,3:T(8,128)(2,1)S(1)} fusion(bf16[36,2,16,64,128]{4,3,2,1,0:T(8,128)(2,1)} %gather_fusion, pred[36]{0:T(512)(128)(4,1)S(1)} %compare_and_fusion.2), kind=kLoop, calls=%fused_computation.7.clone.1 | loop fusion | flops 9437184 | bytes 37748772 | tf_op jit(solution)/shard_map/while/body/eval_jaxpr/jit(_take)/select_n | solution.py:145
  346.9 8.3 %fusion.57 = (bf16[1,16,64,36,128]{4,2,1,0,3:T(8,128)(2,1)}, bf16[1,16,64,36,128]{4,2,1,0,3:T(8,128)(2,1)}) fusion(bf16[2,16,64,36,128]{4,2,1,0,3:T(8,128)(2,1)S(1)} %select_bitcast_fusion.2), kind=kLoop, calls=%fused_computation.98.clone.1 | loop fusion | bytes 37748736 | tf_op jit(solution)/shard_map/while/body/eval_jaxpr/slice | solution.py:147
  355.2 10.7 %copy.112 = bf16[1,16,64,36,128]{4,2,3,1,0:T(8,128)(2,1)} copy(bf16[1,16,64,36,128]{4,2,1,0,3:T(8,128)(2,1)} %get-tuple-element.139) | data formatting | bytes 18874368 | tf_op jit(solution)/shard_map/while/body/eval_jaxpr/slice | solution.py:151
  365.9 10.7 %copy.113 = bf16[1,16,64,36,128]{4,2,3,1,0:T(8,128)(2,1)} copy(bf16[1,16,64,36,128]{4,2,1,0,3:T(8,128)(2,1)} %get-tuple-element.140) | data formatting | bytes 18874368 | tf_op jit(solution)/shard_map/while/body/eval_jaxpr/slice | solution.py:147
  376.5 17.3 %multiply_reduce_fusion.3 = (f32[16,4,128]{2,1,0:T(4,128)S(1)}, f32[16,4,128,9,128]{2,4,3,1,0:T(8,128)}) fusion(bf16[16,64,4,9,128]{4,1,3,2,0:T(8,128)(2,1)} %bitcast.133, bf16[16,64,12,128]{3,1,0,2:T(8,128)(2,1)} %get-tuple-element.168, s32[]{:T(128)S(6)} %select_n.118), kind=kOutput, calls=%fused_computation.5.clone.1 | convolution fusion | flops 1226825728 | bytes 48267268 | tf_op jit(solution)/shard_map/while/body/eval_jaxpr/hdbq,hdbjk->hbqjk/dot_general | solution.py:146
  393.8 16.3 %fusion.58 = f32[16,4,128]{2,1,0:T(4,128)S(1)} fusion(f32[16,4,128,9,128]{2,4,3,1,0:T(8,128)} %get-tuple-element.141, f32[16,4,128]{2,1,0:T(4,128)S(1)} %get-tuple-element.142), kind=kLoop, calls=%fused_computation.6.clone.1 | loop fusion | flops 28303360 | bytes 37814272 | tf_op jit(solution)/shard_map/while/body/eval_jaxpr/reduce_sum | solution.py:149
  410.1 20.1 %fusion.59 = bf16[3,16,64,4,128]{4,2,3,1,0:T(8,128)(2,1)} fusion(bf16[3,16,64,4,128]{4,2,3,1,0:T(8,128)(2,1)} %get-tuple-element.154, s32[]{:T(128)S(6)} %copy.118, bf16[16,64,4,9,128]{4,1,3,2,0:T(8,128)(2,1)} %bitcast.134, f32[16,4,128,9,128]{2,4,3,1,0:T(8,128)} %get-tuple-element.141, f32[16,4,128]{2,1,0:T(4,128)S(1)} %fusion.58, ...), kind=kOutput, calls=%fused_computation.11.clone.1 | convolution fusion | flops 1246232576 | bytes 48300036 | tf_op jit(solution)/shard_map/while/body/eval_jaxpr/hbqjk,hdbjk->hdbq/dot_general | solution.py:150
  431.4 13.8 %gather_fusion = bf16[36,2,16,64,128]{4,3,2,1,0:T(8,128)(2,1)} fusion(bf16[2,16,64,32,128]{4,2,3,1,0:T(8,128)(2,1)} %get-tuple-element.166, s32[1024]{0:T(1024)S(1)} %pad_clamp_fusion.2), kind=kCustom, calls=%fused_computation.clone.1 | custom fusion | bytes 37748880 | tf_op jit(solution)/shard_map/while/body/eval_jaxpr/jit(_take)/gather | solution.py:145
  445.2 9.7 %select_bitcast_fusion.2 = bf16[2,16,64,36,128]{4,2,1,0,3:T(8,128)(2,1)S(1)} fusion(bf16[36,2,16,64,128]{4,3,2,1,0:T(8,128)(2,1)} %gather_fusion, pred[36]{0:T(512)(128)(4,1)S(1)} %compare_and_fusion.2), kind=kLoop, calls=%fused_computation.7.clone.1 | loop fusion | flops 9437184 | bytes 37748772 | tf_op jit(solution)/shard_map/while/body/eval_jaxpr/jit(_take)/select_n | solution.py:145
  454.9 8.3 %fusion.57 = (bf16[1,16,64,36,128]{4,2,1,0,3:T(8,128)(2,1)}, bf16[1,16,64,36,128]{4,2,1,0,3:T(8,128)(2,1)}) fusion(bf16[2,16,64,36,128]{4,2,1,0,3:T(8,128)(2,1)S(1)} %select_bitcast_fusion.2), kind=kLoop, calls=%fused_computation.98.clone.1 | loop fusion | bytes 37748736 | tf_op jit(solution)/shard_map/while/body/eval_jaxpr/slice | solution.py:147
  463.3 10.7 %copy.112 = bf16[1,16,64,36,128]{4,2,3,1,0:T(8,128)(2,1)} copy(bf16[1,16,64,36,128]{4,2,1,0,3:T(8,128)(2,1)} %get-tuple-element.139) | data formatting | bytes 18874368 | tf_op jit(solution)/shard_map/while/body/eval_jaxpr/slice | solution.py:151
  473.9 10.7 %copy.113 = bf16[1,16,64,36,128]{4,2,3,1,0:T(8,128)(2,1)} copy(bf16[1,16,64,36,128]{4,2,1,0,3:T(8,128)(2,1)} %get-tuple-element.140) | data formatting | bytes 18874368 | tf_op jit(solution)/shard_map/while/body/eval_jaxpr/slice | solution.py:147
  484.6 17.3 %multiply_reduce_fusion.3 = (f32[16,4,128]{2,1,0:T(4,128)S(1)}, f32[16,4,128,9,128]{2,4,3,1,0:T(8,128)}) fusion(bf16[16,64,4,9,128]{4,1,3,2,0:T(8,128)(2,1)} %bitcast.133, bf16[16,64,12,128]{3,1,0,2:T(8,128)(2,1)} %get-tuple-element.168, s32[]{:T(128)S(6)} %select_n.118), kind=kOutput, calls=%fused_computation.5.clone.1 | convolution fusion | flops 1226825728 | bytes 48267268 | tf_op jit(solution)/shard_map/while/body/eval_jaxpr/hdbq,hdbjk->hbqjk/dot_general | solution.py:146
  501.9 16.3 %fusion.58 = f32[16,4,128]{2,1,0:T(4,128)S(1)} fusion(f32[16,4,128,9,128]{2,4,3,1,0:T(8,128)} %get-tuple-element.141, f32[16,4,128]{2,1,0:T(4,128)S(1)} %get-tuple-element.142), kind=kLoop, calls=%fused_computation.6.clone.1 | loop fusion | flops 28303360 | bytes 37814272 | tf_op jit(solution)/shard_map/while/body/eval_jaxpr/reduce_sum | solution.py:149
  518.2 20.1 %fusion.59 = bf16[3,16,64,4,128]{4,2,3,1,0:T(8,128)(2,1)} fusion(bf16[3,16,64,4,128]{4,2,3,1,0:T(8,128)(2,1)} %get-tuple-element.154, s32[]{:T(128)S(6)} %copy.118, bf16[16,64,4,9,128]{4,1,3,2,0:T(8,128)(2,1)} %bitcast.134, f32[16,4,128,9,128]{2,4,3,1,0:T(8,128)} %get-tuple-element.141, f32[16,4,128]{2,1,0:T(4,128)S(1)} %fusion.58, ...), kind=kOutput, calls=%fused_computation.11.clone.1 | convolution fusion | flops 1246232576 | bytes 48300036 | tf_op jit(solution)/shard_map/while/body/eval_jaxpr/hbqjk,hdbjk->hdbq/dot_general | solution.py:150
  539.5 13.8 %gather_fusion = bf16[36,2,16,64,128]{4,3,2,1,0:T(8,128)(2,1)} fusion(bf16[2,16,64,32,128]{4,2,3,1,0:T(8,128)(2,1)} %get-tuple-element.166, s32[1024]{0:T(1024)S(1)} %pad_clamp_fusion.2), kind=kCustom, calls=%fused_computation.clone.1 | custom fusion | bytes 37748880 | tf_op jit(solution)/shard_map/while/body/eval_jaxpr/jit(_take)/gather | solution.py:145
  553.3 9.7 %select_bitcast_fusion.2 = bf16[2,16,64,36,128]{4,2,1,0,3:T(8,128)(2,1)S(1)} fusion(bf16[36,2,16,64,128]{4,3,2,1,0:T(8,128)(2,1)} %gather_fusion, pred[36]{0:T(512)(128)(4,1)S(1)} %compare_and_fusion.2), kind=kLoop, calls=%fused_computation.7.clone.1 | loop fusion | flops 9437184 | bytes 37748772 | tf_op jit(solution)/shard_map/while/body/eval_jaxpr/jit(_take)/select_n | solution.py:145
  563.0 8.3 %fusion.57 = (bf16[1,16,64,36,128]{4,2,1,0,3:T(8,128)(2,1)}, bf16[1,16,64,36,128]{4,2,1,0,3:T(8,128)(2,1)}) fusion(bf16[2,16,64,36,128]{4,2,1,0,3:T(8,128)(2,1)S(1)} %select_bitcast_fusion.2), kind=kLoop, calls=%fused_computation.98.clone.1 | loop fusion | bytes 37748736 | tf_op jit(solution)/shard_map/while/body/eval_jaxpr/slice | solution.py:147
  571.3 10.7 %copy.112 = bf16[1,16,64,36,128]{4,2,3,1,0:T(8,128)(2,1)} copy(bf16[1,16,64,36,128]{4,2,1,0,3:T(8,128)(2,1)} %get-tuple-element.139) | data formatting | bytes 18874368 | tf_op jit(solution)/shard_map/while/body/eval_jaxpr/slice | solution.py:151
  582.0 10.7 %copy.113 = bf16[1,16,64,36,128]{4,2,3,1,0:T(8,128)(2,1)} copy(bf16[1,16,64,36,128]{4,2,1,0,3:T(8,128)(2,1)} %get-tuple-element.140) | data formatting | bytes 18874368 | tf_op jit(solution)/shard_map/while/body/eval_jaxpr/slice | solution.py:147
  592.7 17.3 %multiply_reduce_fusion.3 = (f32[16,4,128]{2,1,0:T(4,128)S(1)}, f32[16,4,128,9,128]{2,4,3,1,0:T(8,128)}) fusion(bf16[16,64,4,9,128]{4,1,3,2,0:T(8,128)(2,1)} %bitcast.133, bf16[16,64,12,128]{3,1,0,2:T(8,128)(2,1)} %get-tuple-element.168, s32[]{:T(128)S(6)} %select_n.118), kind=kOutput, calls=%fused_computation.5.clone.1 | convolution fusion | flops 1226825728 | bytes 48267268 | tf_op jit(solution)/shard_map/while/body/eval_jaxpr/hdbq,hdbjk->hbqjk/dot_general | solution.py:146
  610.0 16.3 %fusion.58 = f32[16,4,128]{2,1,0:T(4,128)S(1)} fusion(f32[16,4,128,9,128]{2,4,3,1,0:T(8,128)} %get-tuple-element.141, f32[16,4,128]{2,1,0:T(4,128)S(1)} %get-tuple-element.142), kind=kLoop, calls=%fused_computation.6.clone.1 | loop fusion | flops 28303360 | bytes 37814272 | tf_op jit(solution)/shard_map/while/body/eval_jaxpr/reduce_sum | solution.py:149
  626.3 20.1 %fusion.59 = bf16[3,16,64,4,128]{4,2,3,1,0:T(8,128)(2,1)} fusion(bf16[3,16,64,4,128]{4,2,3,1,0:T(8,128)(2,1)} %get-tuple-element.154, s32[]{:T(128)S(6)} %copy.118, bf16[16,64,4,9,128]{4,1,3,2,0:T(8,128)(2,1)} %bitcast.134, f32[16,4,128,9,128]{2,4,3,1,0:T(8,128)} %get-tuple-element.141, f32[16,4,128]{2,1,0:T(4,128)S(1)} %fusion.58, ...), kind=kOutput, calls=%fused_computation.11.clone.1 | convolution fusion | flops 1246232576 | bytes 48300036 | tf_op jit(solution)/shard_map/while/body/eval_jaxpr/hbqjk,hdbjk->hdbq/dot_general | solution.py:150
  646.6 6.0 copy.86
  652.6 6.1 dot_general.44
  658.7 7.9 %fusion.9 = bf16[1536,1024]{1,0:T(8,128)(2,1)} fusion(f32[1536,1024]{1,0:T(8,128)} %copy-done.3, bf16[1536,64,16]{0,2,1:T(8,128)(2,1)} %dot_general.44, bf16[16,64,1024]{2,1,0:T(8,128)(2,1)S(1)} %bitcast.132), kind=kOutput, calls=%fused_computation.27 | convolution fusion | flops 3224371200 | bytes 14680064 | tf_op jit(solution)/shard_map/nhdgq,hde->ngqe/dot_general | solution.py:156
  (90 shorter events, 29.9 us)
Async XLA Ops:
  0.0 658.7 %copy-start = (bf16[1024,1024]{1,0:T(8,128)(2,1)S(1)}, bf16[1024,1024]{1,0:T(8,128)(2,1)}, u32[]{:S(2)}) copy-start(bf16[1024,1024]{1,0:T(8,128)(2,1)} %param.22) | copy-start | bytes 6291460
  4.8 41.9 %all-to-all-start = ((s32[128,2,1]{1,2,0:T(1,128)}), s32[128,2,1]{1,2,0:T(1,128)S(1)}, u32[]{:S(2)}, u32[]{:S(2)}) async-start(s32[128,2,1]{1,2,0:T(1,128)} %bitcast.16), calls=%async_computation | async-start | bytes 131072 | tf_op jit(solution)/shard_map/all_to_all | solution.py:101
  46.8 110.5 %all-to-all-start.1 = ((bf16[256,128,128]{2,1,0:T(8,128)(2,1)}), bf16[256,128,128]{2,1,0:T(8,128)(2,1)}, u32[]{:S(2)}, u32[]{:S(2)}) async-start(bf16[256,128,128]{2,1,0:T(8,128)(2,1)} %scatter_fusion), calls=%async_computation.1 | async-start | bytes 16777216 | tf_op jit(solution)/shard_map/all_to_all | solution.py:100
  59.7 105.6 %copy-start.15 = (bf16[128,1024]{1,0:T(8,128)(2,1)S(1)}, bf16[128,1024]{1,0:T(8,128)(2,1)}, u32[]{:S(2)}) copy-start(bf16[128,1024]{1,0:T(8,128)(2,1)} %param.17) | copy-start | bytes 786436
  165.3 1.1 copy-start.17
  166.4 2.9 copy-start.3
  166.4 4.5 copy-start.18
  169.3 1.7 copy-start.14
  196.0 4.1 copy-start.1
  200.1 73.9 %copy-start.8 = (bf16[1,16,16,2,6,128]{5,2,1,4,3,0:T(8,128)(2,1)}, bf16[1,16,16,2,6,128]{5,2,1,4,3,0:T(8,128)(2,1)S(1)}, u32[]{:S(2)}) copy-start(bf16[1,16,16,2,6,128]{5,2,1,4,3,0:T(8,128)(2,1)S(1)} %get-tuple-element.79) | copy-start | bytes 2359300
  200.1 73.9 %copy-start.10 = (bf16[1,16,16,2,6,128]{5,2,1,4,3,0:T(8,128)(2,1)}, bf16[1,16,16,2,6,128]{5,2,1,4,3,0:T(8,128)(2,1)S(1)}, u32[]{:S(2)}) copy-start(bf16[1,16,16,2,6,128]{5,2,1,4,3,0:T(8,128)(2,1)S(1)} %get-tuple-element.86) | copy-start | bytes 2359300
  200.1 73.9 %copy-start.12 = (bf16[1,16,16,2,6,128]{5,2,1,4,3,0:T(8,128)(2,1)}, bf16[1,16,16,2,6,128]{5,2,1,4,3,0:T(8,128)(2,1)S(1)}, u32[]{:S(2)}) copy-start(bf16[1,16,16,2,6,128]{5,2,1,4,3,0:T(8,128)(2,1)S(1)} %get-tuple-element.87) | copy-start | bytes 2359300
  203.3 66.7 %collective-permute-start = (bf16[2,16,64,1,6,128]{5,2,1,4,3,0:T(8,128)(2,1)S(1)}, bf16[2,16,64,1,6,128]{5,2,1,4,3,0:T(8,128)(2,1)S(1)}, u32[]{:S(2)}, u32[]{:S(2)}) collective-permute-start(bf16[2,16,64,1,6,128]{5,2,1,4,3,0:T(8,128)(2,1)S(1)} %get-tuple-element.84), channel_id=1, source_target_pairs={{0,32},{32,64},{64,96},{1,33},{33,65},{65,97},{2,34},{34,66},{66,9... | collective-permute-start | bytes 9437192 | tf_op jit(solution)/shard_map/ppermute | solution.py:19
  204.8 79.8 %copy-start.16 = (s32[2,6,9]{2,0,1:T(2,128)S(1)}, s32[2,6,9]{2,0,1:T(2,128)}, u32[]{:S(2)}) copy-start(s32[2,6,9]{2,0,1:T(2,128)} %param.23) | copy-start | bytes 1300
  204.8 69.2 %collective-permute-start.1 = (bf16[2,16,64,1,6,128]{5,2,1,4,3,0:T(8,128)(2,1)S(1)}, bf16[2,16,64,1,6,128]{5,2,1,4,3,0:T(8,128)(2,1)S(1)}, u32[]{:S(2)}, u32[]{:S(2)}) collective-permute-start(bf16[2,16,64,1,6,128]{5,2,1,4,3,0:T(8,128)(2,1)S(1)} %get-tuple-element.85), channel_id=1, source_target_pairs={{32,0},{64,32},{96,64},{33,1},{65,33},{97,65},{34,2},{66,34},{98,6... | collective-permute-start | bytes 9437192 | tf_op jit(solution)/shard_map/ppermute | solution.py:22
  270.0 7.0 %copy-start.4 = (bf16[2,16,64,1,6,128]{5,2,1,4,3,0:T(8,128)(2,1)}, bf16[2,16,64,1,6,128]{5,2,1,4,3,0:T(8,128)(2,1)S(1)}, u32[]{:S(2)}) copy-start(bf16[2,16,64,1,6,128]{5,2,1,4,3,0:T(8,128)(2,1)S(1)} %collective-permute-done) | copy-start | bytes 9437188
  274.1 2.9 copy-start.6
  277.0 30.9 %collective-permute-start.2 = (bf16[2,16,64,4,1,128]{5,2,1,4,3,0:T(8,128)(2,1)}, bf16[2,16,64,4,1,128]{5,2,1,4,3,0:T(8,128)(2,1)}, u32[]{:S(2)}, u32[]{:S(2)}) collective-permute-start(bf16[2,16,64,4,1,128]{5,2,1,4,3,0:T(8,128)(2,1)} %get-tuple-element.72), channel_id=1, source_target_pairs={{0,1},{1,2},{2,3},{3,4},{4,5},{5,6},{6,7},{7,8},{8,9},{9,10},{10,1... | collective-permute-start | bytes 6291464 | tf_op jit(solution)/shard_map/ppermute | solution.py:19
  284.6 25.8 %collective-permute-start.3 = (bf16[2,16,64,4,1,128]{5,2,1,4,3,0:T(8,128)(2,1)}, bf16[2,16,64,4,1,128]{5,2,1,4,3,0:T(8,128)(2,1)}, u32[]{:S(2)}, u32[]{:S(2)}) collective-permute-start(bf16[2,16,64,4,1,128]{5,2,1,4,3,0:T(8,128)(2,1)} %get-tuple-element.73), channel_id=1, source_target_pairs={{1,0},{2,1},{3,2},{4,3},{5,4},{6,5},{7,6},{8,7},{9,8},{10,9},{11,1... | collective-permute-start | bytes 6291464 | tf_op jit(solution)/shard_map/ppermute | solution.py:22
  299.9 10.4 %copy-start.7 = (bf16[2,16,64,1,6,128]{5,2,1,4,3,0:T(8,128)(2,1)S(1)}, bf16[2,16,64,1,6,128]{5,2,1,4,3,0:T(8,128)(2,1)}, u32[]{:S(2)}) copy-start(bf16[2,16,64,1,6,128]{5,2,1,4,3,0:T(8,128)(2,1)} %copy-done.6) | copy-start | bytes 9437188
  299.9 10.4 %copy-start.9 = (bf16[1,16,16,2,6,128]{5,2,1,4,3,0:T(8,128)(2,1)S(1)}, bf16[1,16,16,2,6,128]{5,2,1,4,3,0:T(8,128)(2,1)}, u32[]{:S(2)}) copy-start(bf16[1,16,16,2,6,128]{5,2,1,4,3,0:T(8,128)(2,1)} %copy-done.8) | copy-start | bytes 2359300
  299.9 10.4 %copy-start.11 = (bf16[1,16,16,2,6,128]{5,2,1,4,3,0:T(8,128)(2,1)S(1)}, bf16[1,16,16,2,6,128]{5,2,1,4,3,0:T(8,128)(2,1)}, u32[]{:S(2)}) copy-start(bf16[1,16,16,2,6,128]{5,2,1,4,3,0:T(8,128)(2,1)} %copy-done.10) | copy-start | bytes 2359300
  299.9 10.4 %copy-start.13 = (bf16[1,16,16,2,6,128]{5,2,1,4,3,0:T(8,128)(2,1)S(1)}, bf16[1,16,16,2,6,128]{5,2,1,4,3,0:T(8,128)(2,1)}, u32[]{:S(2)}) copy-start(bf16[1,16,16,2,6,128]{5,2,1,4,3,0:T(8,128)(2,1)} %copy-done.12) | copy-start | bytes 2359300
  304.0 6.4 copy-start.2
  304.0 6.4 copy-start.5
where the time goes:
time: 676 us; the launch traced here: 667 us
  local copies, waits for them, and re-layouts  205 us (30%)
  waiting for transfers between devices  170 us (25%)
  matrix products  157 us (23%)
  other arithmetic  100 us (15%)
  starting transfers between devices  31.7 us (5%)
    all_to_all x1, waiting for transfers between devices, body(): lax.all_to_all(send_parts, ('band', 'sector'), split_axis=0, concat_axis=...  97.6 us
    ppermute x2, waiting for transfers between devices, padded(): lax.ppermute(lax.slice_in_dim(block, block.shape[dim] - width, None, axis...  65.8 us
    dot_general x3, matrix products, attend(): jnp.einsum('hbqjk,hdbjk->hdbq', probs, chosen[1], preferred_element_type=...  60.4 us
    slice x6, local copies, waits for them, and re-layouts, attend(): chosen[0]  56.9 us
    dot_general x3, matrix products, attend(): jnp.einsum('hdbq,hdbjk->hbqjk', query_heads, chosen[0], preferred_element...  51.8 us
    reduce_sum x3, other arithmetic, attend(): probs = jax.nn.softmax(scores, axis=(-2, -1)).astype(jnp.bfloat16)  48.9 us
    gather x3, local copies, waits for them, and re-layouts, attend(): jnp.take(ext_flat, listed, axis=3).reshape(2, HEADS, HD, group, 9, tile)  41.3 us
    slice x3, local copies, waits for them, and re-layouts, attend(): chosen[1]  32.1 us
  transfers between devices with their start and end apart: 6, of which 5 were waited for; matrix products, arithmetic and copies ran while one was open for 8% of the time, Pallas kernels for 0%

commit v1 on v0

v1 whole, which is shorter than its diff:
```python
import math

import jax
import jax.numpy as jnp
import numpy as np
from jax import lax
from jax.experimental import pallas as pl
from jax.experimental.pallas import tpu as pltpu
from jax.sharding import PartitionSpec as P

NOWN, NEXT, TILE, D, C = 12, 32, 128, 1024, 128
GROUP = 4

def mega_kernel(idx_ref, row_ref, col_ref, rem_ref, we_ref, gain_ref, wq_ref, wk_ref, wv_ref, wo_ref,
                cr_ref, cc_ref, sr_ref, sc_ref, out_ref, k_scr, v_scr, q_scr, att_scr, cos_scr, sin_scr):
    lane = lax.broadcasted_iota(jnp.int32, (1, 128), 1)
    is_row = (lane & 63) < 32
    is_low = (lane & 31) < 16
    first = lane < 64
    rows = GROUP * TILE

    def rotary(u):
        parts = []
        partner = jnp.where(is_low, pltpu.roll(u, 112, 1), pltpu.roll(u, 16, 1))
        return u * cos_scr[...] + partner * sin_scr[...]

    def project(g, own):
        base = g * GROUP
        for i in range(GROUP):
            r = row_ref[base + i]
            c = col_ref[base + i]
            cos_scr[pl.ds(i * TILE, TILE), :] = jnp.where(is_row, cr_ref[r], cc_ref[c])
            sin_scr[pl.ds(i * TILE, TILE), :] = jnp.where(is_row, sr_ref[r], sc_ref[c])
        rem = rem_ref[pl.ds(base, GROUP)].reshape(rows, C)
        emb = jnp.dot(rem, we_ref[...], preferred_element_type=jnp.float32)
        ms = jnp.mean(emb * emb, axis=-1, keepdims=True)
        normed = (emb * lax.rsqrt(ms + 1e-05) * gain_ref[...]).astype(jnp.bfloat16)
        for n in range(4):
            cols = slice(n * 256, (n + 1) * 256)
            k = jnp.dot(normed, wk_ref[:, cols], preferred_element_type=jnp.float32)
            for h in range(2):
                kk = rotary(k[:, h * 128:(h + 1) * 128]).astype(jnp.bfloat16)
                k_scr[pl.ds(base, GROUP), :, n * 256 + h * 128: n * 256 + (h + 1) * 128] = kk.reshape(GROUP, TILE, 128)
            v = jnp.dot(normed, wv_ref[:, cols], preferred_element_type=jnp.float32).astype(jnp.bfloat16)
            v_scr[pl.ds(base, GROUP), :, cols] = v.reshape(GROUP, TILE, 256)
            if own:
                q = jnp.dot(normed, wq_ref[:, cols], preferred_element_type=jnp.float32)
                for h in range(2):
                    qq = rotary(q[:, h * 128:(h + 1) * 128]).astype(jnp.bfloat16)
                    qq = qq * jnp.asarray(0.125, jnp.bfloat16)
                    zero = jnp.zeros_like(qq)
                    q_scr[pl.ds(base, GROUP), 2 * n + h, :TILE, :] = jnp.where(first, qq, zero).reshape(GROUP, TILE, 128)
                    q_scr[pl.ds(base, GROUP), 2 * n + h, TILE:, :] = jnp.where(first, zero, qq).reshape(GROUP, TILE, 128)

    lax.fori_loop(0, NOWN // GROUP, lambda g, c: (project(g, True), c)[1], 0)
    lax.fori_loop(NOWN // GROUP, NEXT // GROUP, lambda g, c: (project(g, False), c)[1], 0)

    ones = jnp.ones((9 * TILE, 128), jnp.bfloat16)

    def attend(step, carry):
        t = step >> 3
        p = step & 7
        col = pl.ds(pl.multiple_of(p * 128, 128), 128)
        ids = [idx_ref[t * 9 + j] for j in range(9)]
        kcat = jnp.concatenate([k_scr[i, :, col] for i in ids], axis=0)
        s = lax.dot_general(q_scr[t, p], kcat, (((1,), (1,)), ((), ())), preferred_element_type=jnp.float32)
        m = jnp.max(s, axis=-1, keepdims=True)
        w = jnp.exp(s - m).astype(jnp.bfloat16)
        vcat = jnp.concatenate([v_scr[i, :, col] for i in ids], axis=0)
        o = jnp.dot(w, jnp.concatenate([vcat, ones], axis=1), preferred_element_type=jnp.float32)
        o = o[:, :128] / o[:, 128:]
        att_scr[t, :, col] = jnp.where(first, o[:TILE], o[TILE:]).astype(jnp.bfloat16)
        return carry

    lax.fori_loop(0, NOWN * 8, attend, 0)

    def finish(g, carry):
        base = g * GROUP
        att = att_scr[pl.ds(base, GROUP)].reshape(rows, D)
        rem = rem_ref[pl.ds(base, GROUP)].reshape(rows, C)
        for n in range(4):
            cols = slice(n * 256, (n + 1) * 256)
            o = jnp.dot(att, wo_ref[:, cols], preferred_element_type=jnp.float32)
            o = o + jnp.dot(rem, we_ref[:, cols], preferred_element_type=jnp.float32)
            out_ref[pl.ds(base, GROUP), :, cols] = o.astype(jnp.bfloat16).reshape(GROUP, TILE, 256)
        return carry

    lax.fori_loop(0, NOWN // GROUP, finish, 0)


def mega(idx, row_of, col_of, rem, we, gain, wq, wk, wv, wo, cr, cc, sr, sc):
    smem = pl.BlockSpec(memory_space=pltpu.SMEM)
    vmem = pl.BlockSpec(memory_space=pltpu.VMEM)
    return pl.pallas_call(
        mega_kernel,
        out_shape=jax.ShapeDtypeStruct((NOWN, TILE, D), jnp.bfloat16),
        in_specs=[smem] * 3 + [vmem] * 11,
        out_specs=vmem,
        scratch_shapes=[
            pltpu.VMEM((NEXT, TILE, D), jnp.bfloat16),
            pltpu.VMEM((NEXT, TILE, D), jnp.bfloat16),
            pltpu.VMEM((NOWN, 8, 2 * TILE, 128), jnp.bfloat16),
            pltpu.VMEM((NOWN, TILE, D), jnp.bfloat16),
            pltpu.VMEM((GROUP * TILE, 128), jnp.float32),
            pltpu.VMEM((GROUP * TILE, 128), jnp.float32),
        ],
        compiler_params=pltpu.CompilerParams(vmem_limit_bytes=60 << 20),
    )(idx, row_of, col_of, rem, we, gain, wq, wk, wv, wo, cr, cc, sr, sc)


PLACES = (
    [(r, c) for r in (1, 2) for c in range(1, 7)]
    + [(0, c) for c in range(1, 7)]
    + [(3, c) for c in range(1, 7)]
    + [(r, 0) for r in range(4)]
    + [(r, 7) for r in range(4)]
)


def shift(block, axis, periodic, up):
    count = lax.axis_size(axis)
    pairs = [(i, i + 1) for i in range(count - 1)]
    if periodic:
        pairs.append((count - 1, 0))
    if not up:
        pairs = [(b, a) for a, b in pairs]
    return lax.ppermute(block, axis, pairs)


def with_halo(own):
    above = shift(own[1:], "band", False, True)
    below = shift(own[:1], "band", False, False)
    tall = jnp.concatenate([above, own, below], axis=0)
    west = shift(tall[:, 5:], "sector", True, True)
    east = shift(tall[:, :1], "sector", True, False)
    flat = [x.reshape((-1,) + own.shape[2:]) for x in (own, above, below, west, east)]
    return jnp.concatenate(flat, axis=0)


def tile_slots(neighbours, band_at, sect_at, ncols):
    r = neighbours // ncols - band_at * 2 + 1
    c = jnp.mod(neighbours % ncols - sect_at * 6 + 1, ncols)
    slot = (r - 1) * 6 + c - 1
    slot = jnp.where(r == 0, 11 + c, slot)
    slot = jnp.where(r == 3, 17 + c, slot)
    slot = jnp.where(c == 0, 24 + r, slot)
    return jnp.where(c == 7, 28 + r, slot)


def trig_tables(band_at, sect_at, nrows, ncols):
    freq = jnp.arange(1, 17).astype(jnp.float32)
    rows = (band_at * 2 - 1 + jnp.arange(4)).astype(jnp.float32)
    cols = jnp.mod(sect_at * 6 - 1 + jnp.arange(8), ncols).astype(jnp.float32)
    across = jnp.arange(8).astype(jnp.float32)
    along = jnp.arange(16).astype(jnp.float32)
    theta = math.pi * (rows[:, None] + (across + 0.5) * 16.0 / 128) / nrows
    phi = 2.0 * math.pi * (cols[:, None] + (along + 0.5) / 16.0) / ncols
    theta = theta[..., None] * freq
    phi = phi[..., None] * freq
    sign = jnp.asarray(np.array([-1.0, 1.0] * 4, np.float32))

    def spread_row(t, s):
        t = lax.optimization_barrier(t)[:, :, None, None, :] * s[:, None]
        return jnp.broadcast_to(t, (4, 8, 16, 8, 16)).reshape(4, 128, 128)

    def spread_col(t, s):
        t = lax.optimization_barrier(t)[:, None, :, None, :] * s[:, None]
        return jnp.broadcast_to(t, (8, 8, 16, 8, 16)).reshape(8, 128, 128)

    one = jnp.ones_like(sign)
    return (
        spread_row(jnp.cos(theta), one),
        spread_col(jnp.cos(phi), one),
        spread_row(jnp.sin(theta), sign),
        spread_col(jnp.sin(phi), sign),
    )


def body(
    grid_cells,
    remap_weight,
    remap_dest,
    remap_tile,
    w_embed,
    norm_gain,
    w_query,
    w_key,
    w_value,
    w_out,
    neighbours,
):
    nband = lax.axis_size("band")
    nsect = lax.axis_size("sector")
    ndev = nband * nsect
    blocks, top, rowcells, tile = remap_weight.shape
    chan = grid_cells.shape[2]
    trows, tcols = (neighbours.shape[0], neighbours.shape[1])
    cap = 2
    items = blocks * top
    parts = jnp.einsum(
        "rkct,rcf->rktf", remap_weight, grid_cells, preferred_element_type=jnp.float32
    )
    parts = parts.astype(jnp.bfloat16).reshape(items, tile, chan)
    dest = remap_dest.reshape(-1)
    local = remap_tile.reshape(-1)
    order = jnp.arange(items)
    earlier = (dest[:, None] == dest[None, :]) & (order[None, :] < order[:, None])
    rank = jnp.sum(earlier.astype(jnp.int32), axis=1)
    slot = dest * cap + rank
    send_parts = jnp.zeros((ndev * cap, tile, chan), jnp.bfloat16).at[slot].set(parts)
    send_ids = jnp.full((ndev * cap,), -1, jnp.int32).at[slot].set(local)
    got_parts, got_ids = (
        lax.all_to_all(send_parts, ("band", "sector"), split_axis=0, concat_axis=0, tiled=True),
        lax.all_to_all(send_ids, ("band", "sector"), split_axis=0, concat_axis=0, tiled=True),
    )
    owned = trows * tcols
    select = (got_ids[None, :] == jnp.arange(owned)[:, None]).astype(jnp.bfloat16)
    remapped = jnp.einsum(
        "ls,stc->ltc", select, got_parts, preferred_element_type=jnp.float32
    ).astype(jnp.bfloat16)
    band_at = lax.axis_index("band")
    sect_at = lax.axis_index("sector")
    nrows = trows * nband
    ncols = tcols * nsect
    tiles = with_halo(remapped.reshape(trows, tcols, tile, chan))
    index = tile_slots(neighbours.reshape(owned, 9), band_at, sect_at, ncols).reshape(-1)
    tables = trig_tables(band_at, sect_at, nrows, ncols)
    row_of = jnp.asarray(np.array([r for r, _ in PLACES], np.int32))
    col_of = jnp.asarray(np.array([c for _, c in PLACES], np.int32))
    result = mega(
        index, row_of, col_of, tiles, w_embed, norm_gain.reshape(1, -1),
        w_query, w_key, w_value, w_out, *tables,
    )
    return result.reshape(trows, tcols, tile, -1)


def solution(mesh):
    return jax.shard_map(
        body,
        mesh=mesh,
        in_specs=(
            P(("band", "sector"), None, None),
            P(("band", "sector"), None, None, None),
            P(("band", "sector"), None),
            P(("band", "sector"), None),
            P(),
            P(),
            P(),
            P(),
            P(),
            P(),
            P("band", "sector", None),
        ),
        out_specs=P("band", "sector", None, None),
        check_vma=False,
    )
```

time: 676 us -> 322 us (0.48)
  local copies, waits for them, and re-layouts: 205 us -> 52.1 us
  matrix products: 157 us -> 13.3 us
  Pallas kernels: 0 us -> 133 us
  other arithmetic: 100 us -> 3.24 us
  waiting for transfers between devices: 170 us -> 85.3 us
    dot_general x11 -> x0, matrix products: 143 us -> none  [the longest x3 60.4 us: attend(): jnp.einsum('hbqjk,hdbjk->hdbq', probs, chosen[1], preferred_element_type=...]
    pallas_call x0 -> x1, Pallas kernels: none -> 133 us  [mega(): pl.pallas_call(mega_kernel, out_shape=jax.ShapeDtypeStruct((NOWN, TILE, D...]
    slice x10 -> x1, local copies, waits for them, and re-layouts: 91.2 us -> 0.03 us  [with_halo(): below = shift(own[:1], 'band', False, False)]
    ppermute x4, waiting for transfers between devices: 72.3 us -> 9.26 us  [shift(): return lax.ppermute(block, axis, pairs)]
    reduce_sum x3 -> x0, other arithmetic: 48.9 us -> none  [attend(): probs = jax.nn.softmax(scores, axis=(-2, -1)).astype(jnp.bfloat16)]
    gather x3 -> x0, local copies, waits for them, and re-layouts: 41.3 us -> none  [attend(): jnp.take(ext_flat, listed, axis=3).reshape(2, HEADS, HD, group, 9, tile)]
    select_n x6 -> x1, other arithmetic: 29.3 us -> 0.56 us  [tile_slots(): return jnp.where(c == 7, 28 + r, slot)]
    dot_general x4 -> x0, local copies, waits for them, and re-layouts: 25.6 us -> none  [the longest x2 13.5 us: project_heads(): jnp.einsum('wf,rctw->frct', weight, tiles, preferred_element_type=jnp.flo...]
  transfers between devices with their start and end apart: 6 -> 6, of which waited for: 5 -> 5; matrix products, arithmetic and copies ran while one was open for 8% -> 17% of each run, Pallas kernels for 0% -> 0%
where the time goes in v1:
time: 322 us; the launch traced here: 317 us
  Pallas kernels  133 us (41%)
  waiting for transfers between devices  85.3 us (26%)
  local copies, waits for them, and re-layouts  52.1 us (16%)
  starting transfers between devices  30.5 us (9%)
  matrix products  13.3 us (4%)
  other arithmetic  3.24 us (1%)
    pallas_call x1, Pallas kernels, mega(): pl.pallas_call(mega_kernel, out_shape=jax.ShapeDtypeStruct((NOWN, TILE, D...  133 us
    all_to_all x1, waiting for transfers between devices, body(): lax.all_to_all(send_parts, ('band', 'sector'), split_axis=0, concat_axis=...  76.1 us
    scatter x1, local copies, waits for them, and re-layouts, body(): jnp.zeros((ndev * cap, tile, chan), jnp.bfloat16).at[slot].set(parts)  19.5 us
    all_to_all x1, starting transfers between devices, body(): lax.all_to_all(send_ids, ('band', 'sector'), split_axis=0, concat_axis=0,...  10.8 us
    all_to_all x1, starting transfers between devices, body(): lax.all_to_all(send_parts, ('band', 'sector'), split_axis=0, concat_axis=...  10.3 us
    ppermute x4, starting transfers between devices, shift(): return lax.ppermute(block, axis, pairs)  9.47 us
    ppermute x4, waiting for transfers between devices, shift(): return lax.ppermute(block, axis, pairs)  9.26 us
    dot_general x1, matrix products, body(): jnp.einsum('ls,stc->ltc', select, got_parts, preferred_element_type=jnp.f...  7.91 us
  transfers between devices with their start and end apart: 6, of which 5 were waited for; matrix products, arithmetic and copies ran while one was open for 17% of the time, Pallas kernels for 0%

profile of v1, /device:TPU:3, one launch (start us, length us, event | category | flops | bytes accessed | tf_op | source)
XLA Modules:
  0.0 317.3 jit_solution(12005540174380141178)
XLA Ops:
  0.0 0.8 broadcast_multiply_fusion.2
  0.8 0.8 copy.53
  1.6 0.1 copy.52
  1.7 0.1 mul.107
  1.8 0.1 eq.63
  2.0 0.2 convert_reduce_fusion
  2.2 0.8 copy.54
  2.9 0.1 reshape.209
  3.1 1.0 scatter_custom_fusion
  4.1 0.8 all_to_all.9
  4.8 10.8 %all-to-all-start = ((s32[128,2,1]{1,2,0:T(1,128)}), s32[128,2,1]{1,2,0:T(1,128)S(1)}, u32[]{:S(2)}, u32[]{:S(2)}) async-start(s32[128,2,1]{1,2,0:T(1,128)} %bitcast.2), calls=%async_computation | async-start | bytes 131072 | tf_op jit(solution)/shard_map/all_to_all | solution.py:214
  15.7 5.4 %convolution_convert_fusion = bf16[64,2,128,128]{3,2,1,0:T(8,128)(2,1)} fusion(bf16[64,2,128,128]{3,2,1,0:T(8,128)(2,1)} %param.15, bf16[64,128,128]{2,1,0:T(8,128)(2,1)S(1)} %copy-done), kind=kOutput, calls=%fused_computation.4 | convolution fusion | flops 538968064 | bytes 10485760 | tf_op jit(solution)/shard_map/rkct,rcf->rktf/dot_general | solution.py:200
  21.1 5.4 %broadcast_in_dim.9 = bf16[256,128,128]{2,1,0:T(8,128)(2,1)} broadcast(bf16[]{:T(256)} %constant.95.clone.1), dimensions={} | broadcast | bytes 8388610 | tf_op jit(solution)/shard_map/broadcast_in_dim | solution.py:210
  26.5 19.5 %scatter_fusion = bf16[256,128,128]{2,1,0:T(8,128)(2,1)} fusion(bf16[256,128,128]{2,1,0:T(8,128)(2,1)} %broadcast_in_dim.9, s32[128]{0:T(128)S(1)} %fusion.11, bf16[128,128,128]{2,1,0:T(8,128)(2,1)} %bitcast.42), kind=kCustom, calls=%fused_computation.1 | custom fusion | bytes 12583424 | tf_op jit(solution)/shard_map/scatter | solution.py:210
  46.0 10.3 %all-to-all-start.1 = ((bf16[256,128,128]{2,1,0:T(8,128)(2,1)}), bf16[256,128,128]{2,1,0:T(8,128)(2,1)}, u32[]{:S(2)}, u32[]{:S(2)}) async-start(bf16[256,128,128]{2,1,0:T(8,128)(2,1)} %scatter_fusion), calls=%async_computation.1 | async-start | bytes 16777216 | tf_op jit(solution)/shard_map/all_to_all | solution.py:213
  56.3 0.1 div.31
  56.4 0.1 rem.38
  56.5 0.1 ne.51
  56.7 0.1 add_multiply_fusion
  56.7 0.3 multiply_sine_fusion
  57.1 0.1 broadcast_multiply_fusion
  57.2 2.4 broadcast_in_dim.11
  59.6 3.9 %reshape.203.sc_ref = f32[8,128,128]{2,1,0:T(8,128)} reshape(f32[8,8,16,8,16]{4,3,2,1,0:T(8,128)} %broadcast_in_dim.11) | data formatting | bytes 1048576 | tf_op jit(solution)/shard_map/reshape | solution.py:168
  63.6 2.4 broadcast_in_dim_mul.5
  66.0 3.9 %reshape.201.cc_ref = f32[8,128,128]{2,1,0:T(8,128)} reshape(f32[8,8,16,8,16]{4,3,2,1,0:T(8,128)} %broadcast_in_dim_mul.5) | data formatting | bytes 1048576 | tf_op jit(solution)/shard_map/reshape | solution.py:168
  69.9 0.1 add_multiply_fusion.1
  70.0 0.1 multiply_sine_fusion.1
  70.2 0.1 broadcast_multiply_fusion.1
  70.3 1.5 broadcast_in_dim.10
  71.7 2.8 reshape.202.sr_ref
  74.5 1.5 broadcast_in_dim_mul.4
  75.9 2.8 reshape.200.cr_ref
  78.7 0.5 broadcast.244
  79.2 0.8 reduce.3
  80.0 0.1 eq.67
  80.2 76.1 %all-to-all-done.1 = bf16[256,128,128]{2,1,0:T(8,128)(2,1)} async-done(((bf16[256,128,128]{2,1,0:T(8,128)(2,1)}), bf16[256,128,128]{2,1,0:T(8,128)(2,1)}, u32[]{:S(2)}, u32[]{:S(2)}) %all-to-all-start.1) | async-done | bytes 8388640 | tf_op jit(solution)/shard_map/all_to_all | solution.py:213
  156.2 7.9 %fusion = bf16[12,128,128]{2,0,1:T(8,128)(2,1)S(1)} fusion(bf16[256,128,128]{2,1,0:T(8,128)(2,1)} %all-to-all-done.1, s32[256]{0:T(256)S(1)} %eq.67), kind=kOutput, calls=%fused_computation.2 | convolution fusion | flops 100666368 | bytes 8782848 | tf_op jit(solution)/shard_map/ls,stc->ltc/dot_general | solution.py:218
  164.1 0.2 constant_dynamic-update-slice_fusion
  164.4 1.6 collective-permute-start
  166.0 1.3 collective-permute-start.1
  167.3 0.6 compare_select_fusion.4.idx_ref
  167.9 1.1 collective-permute-done
  169.0 3.8 %collective-permute-done.1 = bf16[1,6,128,128]{3,2,0,1:T(8,128)(2,1)S(1)} collective-permute-done((bf16[1,6,128,128]{3,2,0,1:T(8,128)(2,1)S(1)}, bf16[1,6,128,128]{3,2,0,1:T(8,128)(2,1)S(1)}, u32[]{:S(2)}, u32[]{:S(2)}) %collective-permute-start.1) | collective-permute-done | bytes 196640 | tf_op jit(solution)/shard_map/ppermute | solution.py:127
  172.9 6.5 %collective-permute-start.2 = (bf16[4,1,128,128]{3,2,0,1:T(8,128)(2,1)S(1)}, bf16[4,1,128,128]{3,2,0,1:T(8,128)(2,1)S(1)}, u32[]{:S(2)}, u32[]{:S(2)}) collective-permute-start(bf16[4,1,128,128]{3,2,0,1:T(8,128)(2,1)S(1)} %get-tuple-element.8), channel_id=1, source_target_pairs={{0,1},{1,2},{2,3},{3,4},{4,5},{5,6},{6,7},{7,8},{8,9},{9,10},{10,1... | collective-permute-start | bytes 393224 | tf_op jit(solution)/shard_map/ppermute | solution.py:127
  179.5 1.9 collective-permute-done.2
  181.4 2.4 collective-permute-done.3
  183.8 1.0 copy-done.1
  184.8 132.5 %shard_map.136 = bf16[12,128,1024]{2,1,0:T(8,128)(2,1)} custom-call(s32[108]{0:T(128)} %compare_select_fusion.4.idx_ref, s32[32]{0:T(128)} %constant.102.clone.row_ref, s32[32]{0:T(128)} %constant.103.clone.col_ref, bf16[32,128,128]{2,1,0:T(8,128)(2,1)} %copy-done.1, bf16[128,1024]{1,0:T(8,128)(2,1)} %we_ref.1, f32[1,1024]{1,0:T(1,128)} %bitcast.45, ...), custom_call_target="tpu_custom_call" | custom-call | tf_op jit(solution)/shard_map/pallas_call | solution.py:94
  (26 shorter events, 0.2 us)
Async XLA Ops:
  0.0 15.7 %copy-start = (bf16[64,128,128]{2,1,0:T(8,128)(2,1)S(1)}, bf16[64,128,128]{2,1,0:T(8,128)(2,1)}, u32[]{:S(2)}) copy-start(bf16[64,128,128]{2,1,0:T(8,128)(2,1)} %param.14) | copy-start | bytes 6291460
  4.8 41.2 %all-to-all-start = ((s32[128,2,1]{1,2,0:T(1,128)}), s32[128,2,1]{1,2,0:T(1,128)S(1)}, u32[]{:S(2)}, u32[]{:S(2)}) async-start(s32[128,2,1]{1,2,0:T(1,128)} %bitcast.2), calls=%async_computation | async-start | bytes 131072 | tf_op jit(solution)/shard_map/all_to_all | solution.py:214
  46.0 10.3 %copy-start.2 = (s32[2,6,9]{2,0,1:T(2,128)S(1)}, s32[2,6,9]{2,0,1:T(2,128)}, u32[]{:S(2)}) copy-start(s32[2,6,9]{2,0,1:T(2,128)} %param.24) | copy-start | bytes 1300
  46.0 11.1 %copy-start.3 = (f32[8]{0:T(128)S(1)}, f32[8]{0:T(128)}, u32[]{:S(2)}) copy-start(f32[8]{0:T(128)} %constant.101.clone) | copy-start | bytes 100
  46.0 110.2 %all-to-all-start.1 = ((bf16[256,128,128]{2,1,0:T(8,128)(2,1)}), bf16[256,128,128]{2,1,0:T(8,128)(2,1)}, u32[]{:S(2)}, u32[]{:S(2)}) async-start(bf16[256,128,128]{2,1,0:T(8,128)(2,1)} %scatter_fusion), calls=%async_computation.1 | async-start | bytes 16777216 | tf_op jit(solution)/shard_map/all_to_all | solution.py:213
  164.4 4.6 %collective-permute-start = (bf16[1,6,128,128]{3,2,1,0:T(8,128)(2,1)S(1)}, bf16[1,6,128,128]{3,2,1,0:T(8,128)(2,1)S(1)}, u32[]{:S(2)}, u32[]{:S(2)}) collective-permute-start(bf16[1,6,128,128]{3,2,1,0:T(8,128)(2,1)S(1)} %get-tuple-element.10), channel_id=1, source_target_pairs={{0,32},{32,64},{64,96},{1,33},{33,65},{65,97},{2,34},{34,66},{66,9... | collective-permute-start | bytes 589832 | tf_op jit(solution)/shard_map/ppermute | solution.py:127
  166.0 6.8 %collective-permute-start.1 = (bf16[1,6,128,128]{3,2,0,1:T(8,128)(2,1)S(1)}, bf16[1,6,128,128]{3,2,0,1:T(8,128)(2,1)S(1)}, u32[]{:S(2)}, u32[]{:S(2)}) collective-permute-start(bf16[1,6,128,128]{3,2,0,1:T(8,128)(2,1)S(1)} %get-tuple-element.9), channel_id=1, source_target_pairs={{32,0},{64,32},{96,64},{33,1},{65,33},{97,65},{34,2},{66,34},{98,6... | collective-permute-start | bytes 589832 | tf_op jit(solution)/shard_map/ppermute | solution.py:127
  172.9 8.5 %collective-permute-start.2 = (bf16[4,1,128,128]{3,2,0,1:T(8,128)(2,1)S(1)}, bf16[4,1,128,128]{3,2,0,1:T(8,128)(2,1)S(1)}, u32[]{:S(2)}, u32[]{:S(2)}) collective-permute-start(bf16[4,1,128,128]{3,2,0,1:T(8,128)(2,1)S(1)} %get-tuple-element.8), channel_id=1, source_target_pairs={{0,1},{1,2},{2,3},{3,4},{4,5},{5,6},{6,7},{7,8},{8,9},{9,10},{10,1... | collective-permute-start | bytes 393224 | tf_op jit(solution)/shard_map/ppermute | solution.py:127
  179.4 4.4 %collective-permute-start.3 = (bf16[4,1,128,128]{3,2,0,1:T(8,128)(2,1)S(1)}, bf16[4,1,128,128]{3,2,0,1:T(8,128)(2,1)S(1)}, u32[]{:S(2)}, u32[]{:S(2)}) collective-permute-start(bf16[4,1,128,128]{3,2,0,1:T(8,128)(2,1)S(1)} %get-tuple-element.7), channel_id=1, source_target_pairs={{1,0},{2,1},{3,2},{4,3},{5,4},{6,5},{7,6},{8,7},{9,8},{10,9},{11,1... | collective-permute-start | bytes 393224 | tf_op jit(solution)/shard_map/ppermute | solution.py:127
  183.8 1.0 copy-start.1

commit v2 on v0

v2 whole, which is shorter than its diff:
```python
import functools
import math

import jax
import jax.numpy as jnp
import numpy as np
from jax import lax
from jax.experimental import pallas as pl
from jax.experimental.pallas import tpu as pltpu
from jax.sharding import PartitionSpec as P

NOWN, NEXT, TILE, D, C = 12, 32, 128, 1024, 128
CHUNKS = 4
TOK = TILE // CHUNKS
STRIDE = 37

PLACES = (
    [(r, c) for r in (1, 2) for c in range(1, 7)]
    + [(0, c) for c in range(1, 7)]
    + [(3, c) for c in range(1, 7)]
    + [(r, 0) for r in range(4)]
    + [(r, 7) for r in range(4)]
)


def front_kernel(nband, nsect, item_ref, valid_ref, ids_ref, gain_ref, cr_ref, cc_ref, sr_ref, sc_ref,
                 cells_hbm, weight_hbm, we_hbm, wq_hbm, wk_hbm, wv_hbm,
                 rem_out, q_out, k_out, v_out,
                 cells_ref, weight_ref, we_ref, wq_ref, wk_ref, wv_ref,
                 send_scr, recv_scr, gids_scr, lhs_scr, rem_scr, q_scr, k_scr, v_scr,
                 load_sem, out_sem, send_sem, recv_sem, isend_sem, irecv_sem, hsend_sem, hrecv_sem):
    ndev = nband * nsect
    band, sect = lax.axis_index("band"), lax.axis_index("sector")
    me = band * nsect + sect
    mesh_id = pl.DeviceIdType.MESH
    loads = [
        pltpu.make_async_copy(src, dst, load_sem.at[i])
        for i, (src, dst) in enumerate((
            (cells_hbm, cells_ref), (weight_hbm, weight_ref), (we_hbm, we_ref),
            (wk_hbm, wk_ref), (wv_hbm, wv_ref), (wq_hbm, wq_ref)))
    ]
    loads[0].start()
    loads[1].start()
    barrier = pltpu.get_barrier_semaphore()

    def where_is(i):
        d = lax.rem(me + i * STRIDE, ndev)
        return d, (lax.div(d, nsect), lax.rem(d, nsect))

    def greet(i, carry):
        _, place = where_is(i)
        pl.semaphore_signal(barrier, inc=1, device_id=place, device_id_type=mesh_id)
        return carry

    lax.fori_loop(1, ndev, greet, 0)
    rem_scr[:, NOWN:] = jnp.zeros((CHUNKS, NEXT - NOWN, TOK, C), jnp.bfloat16)
    loads[0].wait()
    loads[1].wait()
    for load in loads[2:]:
        load.start()

    def fill(dst, slot, d):
        for k in range(2):
            item = item_ref[2 * d + k]
            value = lax.dot_general(weight_ref[item], cells_ref[item >> 1], (((0,), (0,)), ((), ())),
                                    preferred_element_type=jnp.float32)
            value = (value * valid_ref[2 * d + k]).astype(jnp.bfloat16)
            for h in range(CHUNKS):
                dst[h, slot, k] = value[h * TOK:(h + 1) * TOK]

    fill(recv_scr, me, me)
    gids_scr[me] = ids_ref[me]

    def make(i):
        d, _ = where_is(i)
        fill(send_scr, d, d)

    def ship(h, i):
        d, place = where_is(i)
        pltpu.make_async_remote_copy(
            src_ref=send_scr.at[h, d], dst_ref=recv_scr.at[h, me],
            send_sem=send_sem.at[h], recv_sem=recv_sem.at[h],
            device_id=place, device_id_type=mesh_id).start()

    def ship_first(i):
        d, place = where_is(i)
        pltpu.make_async_remote_copy(
            src_ref=ids_ref.at[d], dst_ref=gids_scr.at[me], send_sem=isend_sem, recv_sem=irecv_sem,
            device_id=place, device_id_type=mesh_id).start()
        ship(0, i)

    def ship_all(h):
        lax.fori_loop(1, ndev, lambda i, c: (ship(h, i), c)[1], 0)

    make(1)
    make(2)
    pl.semaphore_wait(barrier, ndev - 1)

    def step(i, carry):
        make(i + 2)
        ship_first(i)
        return carry

    lax.fori_loop(1, ndev - 2, step, 0)
    ship_first(ndev - 2)
    ship_first(ndev - 1)
    ship_all(1)

    others = pl.ds(0, ndev - 1)
    pltpu.make_async_copy(gids_scr.at[others], gids_scr.at[others], irecv_sem).wait()
    lane = lax.broadcasted_iota(jnp.int32, (NOWN * 16, 128), 1)
    row = lax.broadcasted_iota(jnp.int32, (NOWN * 16, 128), 0)
    diag = (lane & 15) == (row & 15)
    want = ((row >> 4) + 1).astype(jnp.float32)
    for b in range(ndev // 4):
        named = gids_scr[4 * b] + gids_scr[4 * b + 1] + gids_scr[4 * b + 2] + gids_scr[4 * b + 3]
        hit = jnp.where(diag & (named == want), 1.0, 0.0)
        lhs_scr[:, b * 128:(b + 1) * 128] = hit.astype(jnp.bfloat16)
    for load in loads[2:]:
        load.wait()

    lane = lax.broadcasted_iota(jnp.int32, (1, 128), 1)
    is_row = (lane & 63) < 32
    is_low = (lane & 31) < 16

    north = jnp.maximum(band - 1, 0)
    south = jnp.minimum(band + 1, nband - 1)
    west = lax.rem(sect + nsect - 1, nsect)
    east = lax.rem(sect + 1, nsect)

    def halo(h):
        def send(src, dst, count, place):
            pltpu.make_async_remote_copy(
                src_ref=rem_scr.at[h, pl.ds(src, count)], dst_ref=rem_scr.at[h, pl.ds(dst, count)],
                send_sem=hsend_sem.at[h], recv_sem=hrecv_sem.at[h],
                device_id=place, device_id_type=mesh_id).start()

        send(0, 29, 1, (band, west))
        send(6, 30, 1, (band, west))
        send(5, 25, 1, (band, east))
        send(11, 26, 1, (band, east))

        @pl.when(band > 0)
        def _():
            send(0, 18, 6, (north, sect))
            send(0, 31, 1, (north, west))
            send(5, 27, 1, (north, east))

        @pl.when(band < nband - 1)
        def _():
            send(6, 12, 6, (south, sect))
            send(6, 28, 1, (south, west))
            send(11, 24, 1, (south, east))

    def halo_wait(h, sem):
        def wait(count):
            ref = rem_scr.at[h, pl.ds(0, count)]
            pltpu.make_async_copy(ref, ref, sem).wait()

        inner = (band > 0) & (band < nband - 1)

        @pl.when(inner)
        def _():
            wait(20)

        @pl.when(jnp.logical_not(inner))
        def _():
            wait(12)

    def project(h, base, count):
        rows = count * TOK
        toks = pl.ds(pl.multiple_of(h * TOK, TOK), TOK)
        tiles = slice(base, base + count)
        places = PLACES[base:base + count]
        def spread(row_table, col_table):
            blocks = []
            for r, c in places:
                for g in range(TOK // 16):
                    line = row_table[r, pl.ds(h * (TOK // 16) + g, 1), :]
                    blocks.append(jnp.where(is_row, line, col_table[c]))
            return jnp.concatenate(blocks, axis=0)

        cos, sin = spread(cr_ref, cc_ref), spread(sr_ref, sc_ref)

        def rotary(u):
            partner = jnp.where(is_low, pltpu.roll(u, 112, 1), pltpu.roll(u, 16, 1))
            return u * cos + partner * sin

        rem = rem_scr[h, tiles].reshape(rows, C)
        emb = jnp.dot(rem, we_ref[...], preferred_element_type=jnp.float32)
        ms = jnp.mean(emb * emb, axis=-1, keepdims=True)
        normed = (emb * lax.rsqrt(ms + 1e-05) * gain_ref[...]).astype(jnp.bfloat16)

        def put(dst, pair, value):
            dst[pair, tiles, toks, :] = value.reshape(count, TOK, 128)

        for n in range(4):
            cols = slice(n * 256, (n + 1) * 256)
            k = jnp.dot(normed, wk_ref[:, cols], preferred_element_type=jnp.float32)
            v = jnp.dot(normed, wv_ref[:, cols], preferred_element_type=jnp.float32)
            for p in range(2):
                half = slice(p * 128, (p + 1) * 128)
                put(k_scr, 2 * n + p, rotary(k[:, half]).astype(jnp.bfloat16))
                put(v_scr, 2 * n + p, v[:, half].astype(jnp.bfloat16))
            if base < NOWN:
                q = jnp.dot(normed, wq_ref[:, cols], preferred_element_type=jnp.float32)
                for p in range(2):
                    half = slice(p * 128, (p + 1) * 128)
                    turned = rotary(q[:, half]).astype(jnp.bfloat16)
                    put(q_scr, 2 * n + p, turned * jnp.asarray(0.125, jnp.bfloat16))

    def outs(h):
        toks = pl.ds(pl.multiple_of(h * TOK, TOK), TOK)
        return [
            pltpu.make_async_copy(src.at[:, :, toks, :], dst.at[:, :, toks, :], out_sem.at[h, i])
            for i, (src, dst) in enumerate(((k_scr, k_out), (v_scr, v_out), (q_scr, q_out)))
        ] + [pltpu.make_async_copy(rem_scr.at[h, pl.ds(0, NOWN)], rem_out.at[:, toks, :], out_sem.at[h, 3])]

    def chunk(h, carry):
        pltpu.make_async_copy(recv_scr.at[h, others], recv_scr.at[h, others], recv_sem.at[h]).wait()

        @pl.when(h < CHUNKS - 2)
        def _():
            ship_all(h + 2)

        for b in range(TOK // 32):
            low = recv_scr[h, :, :, b * 32:b * 32 + 16, :].reshape(ndev * 32, 128)
            high = recv_scr[h, :, :, b * 32 + 16:b * 32 + 32, :].reshape(ndev * 32, 128)
            total = jnp.dot(lhs_scr[...], jnp.concatenate([low, high], axis=1),
                            preferred_element_type=jnp.float32).astype(jnp.bfloat16)
            for l in range(NOWN):
                rem_scr[h, l, b * 32:b * 32 + 16, :] = total[l * 16:(l + 1) * 16, :128]
                rem_scr[h, l, b * 32 + 16:b * 32 + 32, :] = total[l * 16:(l + 1) * 16, 128:]
        halo(h)

        @pl.when(h > 0)
        def _():
            for copy in outs(h - 1):
                copy.start()

        project(h, 0, NOWN)
        halo_wait(h, hrecv_sem.at[h])
        project(h, NOWN, NEXT - NOWN)
        return carry

    lax.fori_loop(0, CHUNKS, chunk, 0)
    for copy in outs(CHUNKS - 1):
        copy.start()
    pltpu.make_async_copy(ids_ref.at[others], ids_ref.at[others], isend_sem).wait()
    for h in range(CHUNKS):
        pltpu.make_async_copy(send_scr.at[h, others], send_scr.at[h, others], send_sem.at[h]).wait()
        halo_wait(h, hsend_sem.at[h])
        for copy in outs(h):
            copy.wait()


def front(nband, nsect, item, valid, ids, gain, tables, cells, weights, we, wq, wk, wv):
    ndev = nband * nsect
    smem = pl.BlockSpec(memory_space=pltpu.SMEM)
    vmem = pl.BlockSpec(memory_space=pltpu.VMEM)
    hbm = pl.BlockSpec(memory_space=pltpu.HBM)
    bf16 = jnp.bfloat16
    items, blocks = weights.shape[0], cells.shape[0]
    return pl.pallas_call(
        functools.partial(front_kernel, nband, nsect),
        out_shape=[
            jax.ShapeDtypeStruct((NOWN, TILE, C), bf16),
            jax.ShapeDtypeStruct((8, NOWN, TILE, 128), bf16),
            jax.ShapeDtypeStruct((8, NEXT, TILE, 128), bf16),
            jax.ShapeDtypeStruct((8, NEXT, TILE, 128), bf16),
        ],
        in_specs=[smem, smem] + [vmem] * 6 + [hbm] * 6,
        out_specs=[hbm] * 4,
        scratch_shapes=[
            pltpu.VMEM((blocks, 128, C), bf16),
            pltpu.VMEM((items, 128, TILE), bf16),
            pltpu.VMEM((C, D), bf16),
            pltpu.VMEM((D, D), bf16),
            pltpu.VMEM((D, D), bf16),
            pltpu.VMEM((D, D), bf16),
            pltpu.VMEM((CHUNKS, ndev, 2, TOK, C), bf16),
            pltpu.VMEM((CHUNKS, ndev, 2, TOK, C), bf16),
            pltpu.VMEM((ndev, 1, 128), jnp.float32),
            pltpu.VMEM((NOWN * 16, ndev * 32), bf16),
            pltpu.VMEM((CHUNKS, NEXT, TOK, C), bf16),
            pltpu.VMEM((8, NOWN, TILE, 128), bf16),
            pltpu.VMEM((8, NEXT, TILE, 128), bf16),
            pltpu.VMEM((8, NEXT, TILE, 128), bf16),
            pltpu.SemaphoreType.DMA((6,)),
            pltpu.SemaphoreType.DMA((CHUNKS, 4)),
            pltpu.SemaphoreType.DMA((CHUNKS,)),
            pltpu.SemaphoreType.DMA((CHUNKS,)),
            pltpu.SemaphoreType.DMA,
            pltpu.SemaphoreType.DMA,
            pltpu.SemaphoreType.DMA((CHUNKS,)),
            pltpu.SemaphoreType.DMA((CHUNKS,)),
        ],
        compiler_params=pltpu.CompilerParams(
            collective_id=0, has_side_effects=True, vmem_limit_bytes=63 << 20),
    )(item, valid, ids, gain, *tables, cells, weights, we, wq, wk, wv)


def attend_kernel(idx_ref, q_ref, k_ref, v_ref, rem_ref, we_ref, wo_ref, out_ref, att_scr, s_scr):
    pair = pl.program_id(0)
    first = lax.broadcasted_iota(jnp.int32, (1, 128), 1) < 64
    ones = jnp.ones((9 * TILE, 128), jnp.bfloat16)
    zero = jnp.zeros((TILE, 128), jnp.bfloat16)

    def scores(t, slot):
        q = q_ref[0, t]
        both = jnp.concatenate([jnp.where(first, q, zero), jnp.where(first, zero, q)], axis=0)
        for j in range(9):
            s_scr[slot, :, j * TILE:(j + 1) * TILE] = lax.dot_general(
                both, k_ref[0, idx_ref[t * 9 + j]], (((1,), (1,)), ((), ())),
                preferred_element_type=jnp.float32)

    def combine(t, slot):
        s = s_scr[slot]
        m = jnp.max(s, axis=-1, keepdims=True)
        w = jnp.exp(s - m).astype(jnp.bfloat16)
        near = jnp.concatenate([v_ref[0, idx_ref[t * 9 + j]] for j in range(9)], axis=0)
        o = jnp.dot(w, jnp.concatenate([near, ones], axis=1), preferred_element_type=jnp.float32)
        o = o[:, :128] / o[:, 128:]
        att_scr[pair, t] = jnp.where(first, o[:TILE], o[TILE:]).astype(jnp.bfloat16)

    scores(0, 0)

    def step(half, carry):
        t = half * 2
        scores(t + 1, 1)
        combine(t, 0)
        scores(jnp.minimum(t + 2, NOWN - 1), 0)
        combine(t + 1, 1)
        return carry

    lax.fori_loop(0, NOWN // 2, step, 0)

    @pl.when(pair == 7)
    def _():
        def finish(g, carry):
            base = g * 4
            rows = 4 * TILE
            att = jnp.concatenate(
                [att_scr[p, pl.ds(base, 4)].reshape(rows, 128) for p in range(8)]
                + [rem_ref[pl.ds(base, 4)].reshape(rows, 128)], axis=1)
            for n in range(4):
                cols = slice(n * 256, (n + 1) * 256)
                o = jnp.dot(att[:, :D], wo_ref[:, cols], preferred_element_type=jnp.float32)
                o = o + jnp.dot(att[:, D:], we_ref[:, cols], preferred_element_type=jnp.float32)
                out_ref[pl.ds(base, 4), :, cols] = o.astype(jnp.bfloat16).reshape(4, TILE, 256)
            return carry

        lax.fori_loop(0, NOWN // 4, finish, 0)


def attend(idx, q, k, v, rem, we, wo):
    whole = lambda shape: pl.BlockSpec(shape, lambda p: (0,) * len(shape), pipeline_mode=pl.Buffered(1))
    slab = lambda n: pl.BlockSpec((1, n, TILE, 128), lambda p: (p, 0, 0, 0))
    return pl.pallas_call(
        attend_kernel,
        grid=(8,),
        out_shape=jax.ShapeDtypeStruct((NOWN, TILE, D), jnp.bfloat16),
        in_specs=[
            pl.BlockSpec(memory_space=pltpu.SMEM), slab(NOWN), slab(NEXT), slab(NEXT),
            whole((NOWN, TILE, 128)), whole((128, D)), whole((D, D)),
        ],
        out_specs=whole((NOWN, TILE, D)),
        scratch_shapes=[
            pltpu.VMEM((8, NOWN, TILE, 128), jnp.bfloat16),
            pltpu.VMEM((2, 2 * TILE, 9 * TILE), jnp.float32),
        ],
        compiler_params=pltpu.CompilerParams(vmem_limit_bytes=60 << 20),
    )(idx, q, k, v, rem, we, wo)

def slots(remap_dest, remap_tile, me, ndev):
    dest = remap_dest.reshape(-1)
    named = remap_tile.reshape(-1) + 1
    count = dest.shape[0]
    order = jnp.arange(count)[None, :]
    same = dest[None, :] == jnp.arange(ndev)[:, None]
    first = jnp.min(jnp.where(same, order, count), axis=1)
    last = jnp.max(jnp.where(same, order, -1), axis=1)
    second = jnp.where(last > first, last, count)
    pick = jnp.stack([first, second], axis=1)
    valid = pick < count
    ids = jnp.sum(jnp.where(pick[:, :, None] == order[None], named[None, None, :], 0), axis=2)
    lane = jnp.arange(128)
    mine = (lane >> 5) == (me & 3)
    lanes = jnp.where((lane & 16) == 0, ids[:, :1], ids[:, 1:])
    lanes = jnp.where(mine, lanes, 0).astype(jnp.float32)
    item = jnp.where(valid, pick, 0).reshape(-1)
    return item, valid.astype(jnp.float32).reshape(-1), lanes.reshape(ndev, 1, 128)


def tile_slots(neighbours, band_at, sect_at, ncols):
    r = neighbours // ncols - band_at * 2 + 1
    c = jnp.mod(neighbours % ncols - sect_at * 6 + 1, ncols)
    slot = (r - 1) * 6 + c - 1
    slot = jnp.where(r == 0, 11 + c, slot)
    slot = jnp.where(r == 3, 17 + c, slot)
    slot = jnp.where(c == 0, 24 + r, slot)
    return jnp.where(c == 7, 28 + r, slot)


def trig_tables(band_at, sect_at, nrows, ncols):
    rows = (band_at * 2 - 1 + jnp.arange(4)).astype(jnp.float32)
    cols = jnp.mod(sect_at * 6 - 1 + jnp.arange(8), ncols).astype(jnp.float32)
    across = jnp.arange(8).astype(jnp.float32)
    along = jnp.arange(16).astype(jnp.float32)
    theta = math.pi * (rows[:, None] + (across + 0.5) * 16.0 / 128) / nrows
    phi = 2.0 * math.pi * (cols[:, None] + (along + 0.5) / 16.0) / ncols
    lane = np.arange(128)
    freq = jnp.asarray((lane % 16 + 1).astype(np.float32))
    theta = theta[..., None] * freq
    phi = phi[..., None] * freq
    sign = jnp.asarray(np.where(lane % 32 < 16, -1.0, 1.0).astype(np.float32))
    return jnp.cos(theta), jnp.cos(phi), jnp.sin(theta) * sign, jnp.sin(phi) * sign


def body(
    grid_cells,
    remap_weight,
    remap_dest,
    remap_tile,
    w_embed,
    norm_gain,
    w_query,
    w_key,
    w_value,
    w_out,
    neighbours,
):
    nband = lax.axis_size("band")
    nsect = lax.axis_size("sector")
    ndev = nband * nsect
    blocks, top, rowcells, tile = remap_weight.shape
    trows, tcols = (neighbours.shape[0], neighbours.shape[1])
    owned = trows * tcols
    band_at = lax.axis_index("band")
    sect_at = lax.axis_index("sector")
    item, valid, ids = slots(remap_dest, remap_tile, band_at * nsect + sect_at, ndev)
    tables = trig_tables(band_at, sect_at, trows * nband, tcols * nsect)
    index = tile_slots(neighbours.reshape(owned, 9), band_at, sect_at, tcols * nsect).reshape(-1)
    rem, q, k, v = front(
        nband, nsect, item, valid, ids, norm_gain.reshape(1, -1), tables,
        grid_cells, remap_weight.reshape(blocks * top, rowcells, tile), w_embed, w_query, w_key, w_value,
    )
    result = attend(index, q, k, v, rem, w_embed, w_out)
    return result.reshape(trows, tcols, tile, -1)


def solution(mesh):
    return jax.shard_map(
        body,
        mesh=mesh,
        in_specs=(
            P(("band", "sector"), None, None),
            P(("band", "sector"), None, None, None),
            P(("band", "sector"), None),
            P(("band", "sector"), None),
            P(),
            P(),
            P(),
            P(),
            P(),
            P(),
            P("band", "sector", None),
        ),
        out_specs=P("band", "sector", None, None),
        check_vma=False,
    )
```

time: 676 us -> 207 us (0.31)
  local copies, waits for them, and re-layouts: 205 us -> 1.66 us
  Pallas kernels: 0 us -> 193 us
  waiting for transfers between devices: 170 us -> 0 us
  matrix products: 157 us -> 0 us
  other arithmetic: 100 us -> 8.36 us
  starting transfers between devices: 31.7 us -> 0 us
    pallas_call x0 -> x2, Pallas kernels: none -> 193 us  [the longest x1 139 us: front(): pl.pallas_call(functools.partial(front_kernel, nband, nsect), out_shape=[...]
    dot_general x13 -> x0, matrix products: 157 us -> none  [the longest x3 60.4 us: attend(): jnp.einsum('hbqjk,hdbjk->hdbq', probs, chosen[1], preferred_element_type=...]
    all_to_all x2 -> x0, waiting for transfers between devices: 97.6 us -> none  [the longest x1 97.6 us: body(): lax.all_to_all(send_parts, ('band', 'sector'), split_axis=0, concat_axis=...]
    slice x10 -> x1, local copies, waits for them, and re-layouts: 91.2 us -> 0.01 us  [slots(): lanes = jnp.where(lane & 16 == 0, ids[:, :1], ids[:, 1:])]
    ppermute x4 -> x0, waiting for transfers between devices: 72.3 us -> none  [the longest x2 65.8 us: padded(): lax.ppermute(lax.slice_in_dim(block, block.shape[dim] - width, None, axis...]
    reduce_sum x4 -> x1, other arithmetic: 49.1 us -> 0.18 us  [slots(): jnp.sum(jnp.where(pick[:, :, None] == order[None], named[None, None, :],...]
    gather x3 -> x0, local copies, waits for them, and re-layouts: 41.3 us -> none  [attend(): jnp.take(ext_flat, listed, axis=3).reshape(2, HEADS, HD, group, 9, tile)]
    select_n x7 -> x3, other arithmetic: 29.3 us -> 1.18 us  [the longest x1 0.62 us: tile_slots(): return jnp.where(c == 7, 28 + r, slot)]
  transfers between devices with their start and end apart: 6 -> 0, of which waited for: 5 -> 0; matrix products, arithmetic and copies ran while one was open for 8% -> 0% of each run, Pallas kernels for 0% -> 0%
where the time goes in v2:
time: 207 us; the launch traced here: 203 us
  Pallas kernels  193 us (93%)
  other arithmetic  8.36 us (4%)
    pallas_call x1, Pallas kernels, front(): pl.pallas_call(functools.partial(front_kernel, nband, nsect), out_shape=[...  139 us
    pallas_call x1, Pallas kernels, attend(): pl.pallas_call(attend_kernel, grid=(8,), out_shape=jax.ShapeDtypeStruct((...  54 us

profile of v2, /device:TPU:3, one launch (start us, length us, event | category | flops | bytes accessed | tf_op | source)
XLA Modules:
  0.0 203.1 jit_solution(7796905331457931451)
XLA Ops:
  0.1 0.1 add_multiply_fusion.1
  0.1 0.7 broadcast_add_fusion
  0.8 0.1 add_multiply_fusion
  0.9 0.7 sign_compare_fusion
  1.6 0.1 ne.51
  1.7 0.7 broadcast_divide_fusion
  2.4 0.1 div.31
  2.5 0.1 rem.38
  2.6 0.6 compare_select_fusion.5.idx_ref
  3.2 1.4 fusion.2
  4.6 0.1 copy.32
  4.7 0.1 add.176
  4.9 0.8 copy.30
  5.6 0.1 eq.73
  5.8 0.1 select_reduce_fusion.2
  5.9 0.2 select_reduce_fusion
  6.1 1.0 fusion.1.ids_ref
  7.1 0.1 copy.31
  7.2 0.1 stack.11
  7.3 0.6 compare_select_fusion.1.item_ref
  7.9 0.6 compare_convert_fusion.valid_ref
  8.5 1.6 fusion
  10.1 139.0 %shard_map.127 = (bf16[12,128,128]{2,1,0:T(8,128)(2,1)}, bf16[8,12,128,128]{3,2,1,0:T(8,128)(2,1)}, bf16[8,32,128,128]{3,2,1,0:T(8,128)(2,1)}, bf16[8,32,128,128]{3,2,1,0:T(8,128)(2,1)}) custom-call(s32[256]{0:T(256)} %compare_select_fusion.1.item_ref, f32[256]{0:T(256)} %compare_convert_fusion.valid_ref, f32[128,1,128]{2,1,0:T(1,128)} %fusion.1.ids_ref, ...), custom_call_target="tpu_custom_call" | custom-call | tf_op jit(solution)/shard_map/pallas_call | solution.py:264
  149.1 54.0 %shard_map.128 = bf16[12,128,1024]{2,1,0:T(8,128)(2,1)} custom-call(s32[108]{0:T(128)} %compare_select_fusion.5.idx_ref, bf16[8,12,128,128]{3,2,1,0:T(8,128)(2,1)} %get-tuple-element.9.q_ref, bf16[8,32,128,128]{3,2,1,0:T(8,128)(2,1)} %get-tuple-element.10.k_ref, bf16[8,32,128,128]{3,2,1,0:T(8,128)(2,1)} %get-tuple-element.11.v_ref, ...), custom_call_target="tpu_custom_call" | custom-call | tf_op jit(solution)/shard_map/pallas_call | solution.py:359
  (11 shorter events, 0.1 us)

commit v3 on v2

--- a/solution.py
+++ b/solution.py
@@ -23,13 +23,14 @@
 )
 
 
-def front_kernel(nband, nsect, item_ref, valid_ref, ids_ref, gain_ref, cr_ref, cc_ref, sr_ref, sc_ref,
+def front_kernel(nband, nsect, item_ref, ids_ref, gain_ref, cos_ref, sin_ref,
                  cells_hbm, weight_hbm, we_hbm, wq_hbm, wk_hbm, wv_hbm,
                  rem_out, q_out, k_out, v_out,
                  cells_ref, weight_ref, we_ref, wq_ref, wk_ref, wv_ref,
                  send_scr, recv_scr, gids_scr, lhs_scr, rem_scr, q_scr, k_scr, v_scr,
                  load_sem, out_sem, send_sem, recv_sem, isend_sem, irecv_sem, hsend_sem, hrecv_sem):
     ndev = nband * nsect
+    items = weight_hbm.shape[0]
     band, sect = lax.axis_index("band"), lax.axis_index("sector")
     me = band * nsect + sect
     mesh_id = pl.DeviceIdType.MESH
@@ -61,10 +62,12 @@
 
     def fill(dst, slot, d):
         for k in range(2):
-            item = item_ref[2 * d + k]
+            slot_item = item_ref[2 * d + k]
+            used = jnp.where(slot_item < items, 1.0, 0.0)
+            item = jnp.minimum(slot_item, items - 1)
             value = lax.dot_general(weight_ref[item], cells_ref[item >> 1], (((0,), (0,)), ((), ())),
                                     preferred_element_type=jnp.float32)
-            value = (value * valid_ref[2 * d + k]).astype(jnp.bfloat16)
+            value = (value * used).astype(jnp.bfloat16)
             for h in range(CHUNKS):
                 dst[h, slot, k] = value[h * TOK:(h + 1) * TOK]
 
@@ -88,6 +91,7 @@
             src_ref=ids_ref.at[d], dst_ref=gids_scr.at[me], send_sem=isend_sem, recv_sem=irecv_sem,
             device_id=place, device_id_type=mesh_id).start()
         ship(0, i)
+        ship(1, i)
 
     def ship_all(h):
         lax.fori_loop(1, ndev, lambda i, c: (ship(h, i), c)[1], 0)
@@ -104,7 +108,7 @@
     lax.fori_loop(1, ndev - 2, step, 0)
     ship_first(ndev - 2)
     ship_first(ndev - 1)
-    ship_all(1)
+    ship_all(2)
 
     others = pl.ds(0, ndev - 1)
     pltpu.make_async_copy(gids_scr.at[others], gids_scr.at[others], irecv_sem).wait()
@@ -169,18 +173,18 @@
 
     def project(h, base, count):
         rows = count * TOK
-        toks = pl.ds(pl.multiple_of(h * TOK, TOK), TOK)
+        toks = pl.ds(h * TOK, TOK)
         tiles = slice(base, base + count)
         places = PLACES[base:base + count]
-        def spread(row_table, col_table):
+        def spread(table):
             blocks = []
             for r, c in places:
                 for g in range(TOK // 16):
-                    line = row_table[r, pl.ds(h * (TOK // 16) + g, 1), :]
-                    blocks.append(jnp.where(is_row, line, col_table[c]))
+                    line = table[pl.ds(r * 8 + h * (TOK // 16) + g, 1), :]
+                    blocks.append(jnp.where(is_row, line, table[32 + c * 16:48 + c * 16, :]))
             return jnp.concatenate(blocks, axis=0)
 
-        cos, sin = spread(cr_ref, cc_ref), spread(sr_ref, sc_ref)
+        cos, sin = spread(cos_ref), spread(sin_ref)
 
         def rotary(u):
             partner = jnp.where(is_low, pltpu.roll(u, 112, 1), pltpu.roll(u, 16, 1))
@@ -209,20 +213,26 @@
                     turned = rotary(q[:, half]).astype(jnp.bfloat16)
                     put(q_scr, 2 * n + p, turned * jnp.asarray(0.125, jnp.bfloat16))
 
-    def outs(h):
-        toks = pl.ds(pl.multiple_of(h * TOK, TOK), TOK)
-        return [
-            pltpu.make_async_copy(src.at[:, :, toks, :], dst.at[:, :, toks, :], out_sem.at[h, i])
-            for i, (src, dst) in enumerate(((k_scr, k_out), (v_scr, v_out), (q_scr, q_out)))
-        ] + [pltpu.make_async_copy(rem_scr.at[h, pl.ds(0, NOWN)], rem_out.at[:, toks, :], out_sem.at[h, 3])]
-
-    def chunk(h, carry):
+    def outs(h, own):
+        toks = pl.ds(h * TOK, TOK)
+        tiles = pl.ds(0, NOWN) if own else pl.ds(NOWN, NEXT - NOWN)
+        pairs = [(s.at[:, tiles, toks, :], o.at[:, tiles, toks, :]) for s, o in ((k_scr, k_out), (v_scr, v_out))]
+        if own:
+            pairs.append((q_scr.at[:, :, toks, :], q_out.at[:, :, toks, :]))
+            pairs.append((rem_scr.at[h, tiles], rem_out.at[:, toks, :]))
+        first = 0 if own else 4
+        return [pltpu.make_async_copy(s, o, out_sem.at[h, first + i]) for i, (s, o) in enumerate(pairs)]
+
+    pending = []
+
+    def flush():
+        for copies in pending:
+            for copy in copies:
+                copy.start()
+        pending.clear()
+
+    def own_part(h):
         pltpu.make_async_copy(recv_scr.at[h, others], recv_scr.at[h, others], recv_sem.at[h]).wait()
-
-        @pl.when(h < CHUNKS - 2)
-        def _():
-            ship_all(h + 2)
-
         for b in range(TOK // 32):
             low = recv_scr[h, :, :, b * 32:b * 32 + 16, :].reshape(ndev * 32, 128)
             high = recv_scr[h, :, :, b * 32 + 16:b * 32 + 32, :].reshape(ndev * 32, 128)
@@ -231,30 +241,37 @@
             for l in range(NOWN):
                 rem_scr[h, l, b * 32:b * 32 + 16, :] = total[l * 16:(l + 1) * 16, :128]
                 rem_scr[h, l, b * 32 + 16:b * 32 + 32, :] = total[l * 16:(l + 1) * 16, 128:]
+        flush()
         halo(h)
-
-        @pl.when(h > 0)
-        def _():
-            for copy in outs(h - 1):
-                copy.start()
-
+        if h == 0:
+            ship_all(3)
         project(h, 0, NOWN)
+        pending.append(outs(h, True))
+
+    def halo_part(h):
         halo_wait(h, hrecv_sem.at[h])
         project(h, NOWN, NEXT - NOWN)
-        return carry
-
-    lax.fori_loop(0, CHUNKS, chunk, 0)
-    for copy in outs(CHUNKS - 1):
-        copy.start()
+        flush()
+        pending.append(outs(h, False))
+
+    own_part(0)
+    own_part(1)
+    own_part(2)
+    halo_part(0)
+    own_part(3)
+    halo_part(1)
+    halo_part(2)
+    halo_part(3)
+    flush()
     pltpu.make_async_copy(ids_ref.at[others], ids_ref.at[others], isend_sem).wait()
     for h in range(CHUNKS):
         pltpu.make_async_copy(send_scr.at[h, others], send_scr.at[h, others], send_sem.at[h]).wait()
         halo_wait(h, hsend_sem.at[h])
-        for copy in outs(h):
+        for copy in outs(h, True) + outs(h, False):
             copy.wait()
 
 
-def front(nband, nsect, item, valid, ids, gain, tables, cells, weights, we, wq, wk, wv):
+def front(nband, nsect, item, ids, gain, tables, cells, weights, we, wq, wk, wv):
     ndev = nband * nsect
     smem = pl.BlockSpec(memory_space=pltpu.SMEM)
     vmem = pl.BlockSpec(memory_space=pltpu.VMEM)
@@ -269,7 +286,7 @@
             jax.ShapeDtypeStruct((8, NEXT, TILE, 128), bf16),
             jax.ShapeDtypeStruct((8, NEXT, TILE, 128), bf16),
         ],
-        in_specs=[smem, smem] + [vmem] * 6 + [hbm] * 6,
+        in_specs=[smem] + [vmem] * 4 + [hbm] * 6,
         out_specs=[hbm] * 4,
         scratch_shapes=[
             pltpu.VMEM((blocks, 128, C), bf16),
@@ -287,7 +304,7 @@
             pltpu.VMEM((8, NEXT, TILE, 128), bf16),
             pltpu.VMEM((8, NEXT, TILE, 128), bf16),
             pltpu.SemaphoreType.DMA((6,)),
-            pltpu.SemaphoreType.DMA((CHUNKS, 4)),
+            pltpu.SemaphoreType.DMA((CHUNKS, 6)),
             pltpu.SemaphoreType.DMA((CHUNKS,)),
             pltpu.SemaphoreType.DMA((CHUNKS,)),
             pltpu.SemaphoreType.DMA,
@@ -297,7 +314,7 @@
         ],
         compiler_params=pltpu.CompilerParams(
             collective_id=0, has_side_effects=True, vmem_limit_bytes=63 << 20),
-    )(item, valid, ids, gain, *tables, cells, weights, we, wq, wk, wv)
+    )(item, ids, gain, *tables, cells, weights, we, wq, wk, wv)
 
 
 def attend_kernel(idx_ref, q_ref, k_ref, v_ref, rem_ref, we_ref, wo_ref, out_ref, att_scr, s_scr):
@@ -382,19 +399,21 @@
     last = jnp.max(jnp.where(same, order, -1), axis=1)
     second = jnp.where(last > first, last, count)
     pick = jnp.stack([first, second], axis=1)
-    valid = pick < count
     ids = jnp.sum(jnp.where(pick[:, :, None] == order[None], named[None, None, :], 0), axis=2)
     lane = jnp.arange(128)
     mine = (lane >> 5) == (me & 3)
     lanes = jnp.where((lane & 16) == 0, ids[:, :1], ids[:, 1:])
     lanes = jnp.where(mine, lanes, 0).astype(jnp.float32)
-    item = jnp.where(valid, pick, 0).reshape(-1)
-    return item, valid.astype(jnp.float32).reshape(-1), lanes.reshape(ndev, 1, 128)
+    return pick.reshape(-1), lanes.reshape(ndev, 1, 128)
 
 
 def tile_slots(neighbours, band_at, sect_at, ncols):
-    r = neighbours // ncols - band_at * 2 + 1
-    c = jnp.mod(neighbours % ncols - sect_at * 6 + 1, ncols)
+    past = neighbours - (band_at * 2 - 1) * ncols
+    r = jnp.zeros_like(past)
+    for edge in range(1, 4):
+        r = r + (past >= edge * ncols).astype(jnp.int32)
+    c = past - r * ncols - (sect_at * 6 - 1)
+    c = jnp.where(c < 0, c + ncols, jnp.where(c >= ncols, c - ncols, c))
     slot = (r - 1) * 6 + c - 1
     slot = jnp.where(r == 0, 11 + c, slot)
     slot = jnp.where(r == 3, 17 + c, slot)
@@ -403,18 +422,19 @@
 
 
 def trig_tables(band_at, sect_at, nrows, ncols):
-    rows = (band_at * 2 - 1 + jnp.arange(4)).astype(jnp.float32)
-    cols = jnp.mod(sect_at * 6 - 1 + jnp.arange(8), ncols).astype(jnp.float32)
-    across = jnp.arange(8).astype(jnp.float32)
-    along = jnp.arange(16).astype(jnp.float32)
-    theta = math.pi * (rows[:, None] + (across + 0.5) * 16.0 / 128) / nrows
-    phi = 2.0 * math.pi * (cols[:, None] + (along + 0.5) / 16.0) / ncols
-    lane = np.arange(128)
-    freq = jnp.asarray((lane % 16 + 1).astype(np.float32))
-    theta = theta[..., None] * freq
-    phi = phi[..., None] * freq
-    sign = jnp.asarray(np.where(lane % 32 < 16, -1.0, 1.0).astype(np.float32))
-    return jnp.cos(theta), jnp.cos(phi), jnp.sin(theta) * sign, jnp.sin(phi) * sign
+    line = jnp.arange(160)[:, None]
+    lane = jnp.arange(128)[None, :]
+    freq = ((lane & 15) + 1).astype(jnp.float32)
+    row = (band_at * 2 - 1 + (line >> 3)).astype(jnp.float32)
+    across = (line & 7).astype(jnp.float32)
+    theta = math.pi * (row + (across + 0.5) * 16.0 / 128) / nrows
+    col = sect_at * 6 - 1 + ((line - 32) >> 4)
+    col = jnp.where(col < 0, col + ncols, jnp.where(col >= ncols, col - ncols, col)).astype(jnp.float32)
+    along = (line & 15).astype(jnp.float32)
+    phi = 2.0 * math.pi * (col + (along + 0.5) / 16.0) / ncols
+    angle = jnp.where(line < 32, theta, phi) * freq
+    sign = jnp.where((lane & 31) < 16, -1.0, 1.0)
+    return jnp.cos(angle), jnp.sin(angle) * sign
 
 
 def body(
@@ -438,11 +458,11 @@
     owned = trows * tcols
     band_at = lax.axis_index("band")
     sect_at = lax.axis_index("sector")
-    item, valid, ids = slots(remap_dest, remap_tile, band_at * nsect + sect_at, ndev)
+    item, ids = slots(remap_dest, remap_tile, band_at * nsect + sect_at, ndev)
     tables = trig_tables(band_at, sect_at, trows * nband, tcols * nsect)
     index = tile_slots(neighbours.reshape(owned, 9), band_at, sect_at, tcols * nsect).reshape(-1)
     rem, q, k, v = front(
-        nband, nsect, item, valid, ids, norm_gain.reshape(1, -1), tables,
+        nband, nsect, item, ids, norm_gain.reshape(1, -1), tables,
         grid_cells, remap_weight.reshape(blocks * top, rowcells, tile), w_embed, w_query, w_key, w_value,
     )
     result = attend(index, q, k, v, rem, w_embed, w_out)

time: 207 us -> 191 us (0.923); the launches traced: 203 us -> 190 us
  Pallas kernels: 193 us -> 184 us
  other arithmetic: 8.36 us -> 4.26 us
    pallas_call x1, Pallas kernels: 139 us -> 130 us  [front(): pl.pallas_call(functools.partial(front_kernel, nband, nsect), out_shape=[...]
where the time goes in v3:
time: 191 us; the launch traced here: 190 us
  Pallas kernels  184 us (96%)
  other arithmetic  4.26 us (2%)
  local copies, waits for them, and re-layouts  2.08 us (1%)
    pallas_call x1, Pallas kernels, front(): pl.pallas_call(functools.partial(front_kernel, nband, nsect), out_shape=[...  130 us
    pallas_call x1, Pallas kernels, attend(): pl.pallas_call(attend_kernel, grid=(8,), out_shape=jax.ShapeDtypeStruct((...  54 us

profile of v3, /device:TPU:3, one launch (start us, length us, event | category | flops | bytes accessed | tf_op | source)
XLA Modules:
  0.0 190.4 jit_solution(3683235924926916736)
XLA Ops:
  0.0 0.7 broadcast_add_fusion
  0.7 0.7 broadcast_subtract_fusion
  1.4 0.1 sub.47
  1.5 0.5 compare_select_fusion.9.idx_ref
  2.1 0.1 copy.24
  2.2 0.1 add.168
  2.3 0.8 copy.22
  3.1 0.1 eq.68
  3.2 0.1 select_reduce_fusion.2
  3.4 0.2 select_reduce_fusion
  3.5 1.0 fusion.1.ids_ref
  4.5 0.1 copy.23
  4.6 0.7 reshape.217.item_ref
  5.4 1.0 fusion
  6.4 130.0 %shard_map.109 = (bf16[12,128,128]{2,1,0:T(8,128)(2,1)}, bf16[8,12,128,128]{3,2,1,0:T(8,128)(2,1)}, bf16[8,32,128,128]{3,2,1,0:T(8,128)(2,1)}, bf16[8,32,128,128]{3,2,1,0:T(8,128)(2,1)}) custom-call(s32[256]{0:T(256)} %reshape.217.item_ref, f32[128,1,128]{2,1,0:T(1,128)} %fusion.1.ids_ref, f32[1,1024]{1,0:T(1,128)} %bitcast.12, ...), custom_call_target="tpu_custom_call" | custom-call | tf_op jit(solution)/shard_map/pallas_call | solution.py:281
  136.4 54.0 %shard_map.110 = bf16[12,128,1024]{2,1,0:T(8,128)(2,1)} custom-call(s32[108]{0:T(128)} %compare_select_fusion.9.idx_ref, bf16[8,12,128,128]{3,2,1,0:T(8,128)(2,1)} %get-tuple-element.9.q_ref, bf16[8,32,128,128]{3,2,1,0:T(8,128)(2,1)} %get-tuple-element.10.k_ref, bf16[8,32,128,128]{3,2,1,0:T(8,128)(2,1)} %get-tuple-element.11.v_ref, ...), custom_call_target="tpu_custom_call" | custom-call | tf_op jit(solution)/shard_map/pallas_call | solution.py:376
  (8 shorter events, 0.1 us)
